TPU v7x, 256 devices: a whole 4x4x8 slice. The times are simulated.
256 devices in a mesh: drive: 4 (over y), brick: 64 (over x, z, core).
Axes of the slice: x: 4, y: 4, z: 8, core: 2. Of those that a mesh axis runs over, the one named last changes fastest.
Arguments:
- cam_tiles: bfloat16 [4, 1, 256, 64, 256], P('drive', None, 'brick')
- vox_embed: bfloat16 [1536, 128, 256], P('brick'), may hold values from -6 to 6
- prev_state: bfloat16 [4, 1536, 128, 256], P('drive', 'brick'), may hold values from -6 to 6
- tile_sends: int32 [4, 1, 64, 128], P('drive', None, 'brick'), may hold values from 0 to 3, as said below
- brick_tiles: int32 [4, 1, 1536, 8], P('drive', None, 'brick'), may hold values from -1 to 127, as said below
- ego_shift: int32 [4, 1], P('drive'), may hold values from 0 to 24
- norm_gains: float32 [2, 256], replicated, may hold values from 0.1 to 1.9
- w_query: bfloat16 [256, 256], replicated, may hold values from -0.375 to 0.375
- w_keyval: bfloat16 [256, 512], replicated, may hold values from -0.375 to 0.375
- w_attn_out: bfloat16 [256, 256], replicated, may hold values from -0.375 to 0.375
- w_in: bfloat16 [256, 512], replicated, may hold values from -0.375 to 0.375
- w_out: bfloat16 [512, 256], replicated, may hold values from -0.25 to 0.25
- grad_out: bfloat16 [4, 1536, 128, 256], P('drive', 'brick'), may hold values from -0.015625 to 0.015625
Outputs:
- new_state: bfloat16 [4, 1536, 128, 256], P('drive', 'brick')
- grad_w_in: float32 [256, 512], replicated
- grad_w_out: float32 [512, 256], replicated
Inputs may be any that keep to these rules, and one draw needn't show every extreme that they name: `tile_sends`: entry [drive, frame, p, d * 2 + c] is a tile of shard p, a local index, that shard p sends to shard d as its c-th slot; the 2 entries of one pair are distinct. `brick_tiles`: -1 is padding; other entries are distinct within a brick and name received slots; every brick has one or more, and in each drive and frame some brick has all 8.
All inputs are finite; a program needn't handle non-finite values.
Results may differ from a plain program's by a relative error of at most 0.0022.
The roundings to bfloat16 on the way count: a program that leaves them out, or rounds other values in their place, can miss the bound.
Values may be sent and summed in bfloat16 or wider, within the bound.
No kernel may reach another device: no remote copies, remote signals or barrier semaphores. Data moves between devices by JAX's collectives and lax.ppermute only.
A program may use at most 128 MiB of HBM per device.

v0:
```python
import jax
import jax.numpy as jnp
from jax import lax
from jax.sharding import PartitionSpec as P

HD = 32


def passed_along(value, axis, by):
    count = lax.axis_size(axis)
    pairs = [(i, i + by) for i in range(count) if 0 <= i + by < count]
    return lax.ppermute(value, axis, pairs)


def rms_norm(values, norm_gain):
    mean_sq = jnp.mean(values * values, axis=-1, keepdims=True)
    return values * lax.rsqrt(mean_sq + 1e-06) * norm_gain


def gelu_tanh(values):
    return jax.nn.gelu(values, approximate=True)


def take_rows(source_rows, positions):
    return source_rows[positions]


def on_device(
    cam_tiles,
    vox_embed,
    prev_state,
    tile_sends,
    brick_tiles,
    ego_shift,
    norm_gains,
    w_query,
    w_keyval,
    w_attn_out,
    w_in,
    w_out,
    grad_out,
):
    shards = lax.axis_size("brick")
    own_index = lax.axis_index("brick")
    frames = cam_tiles.shape[1]
    tile_dev = cam_tiles.shape[2]
    pixels = cam_tiles.shape[3]
    width = cam_tiles.shape[4]
    slots = tile_sends.shape[3]
    capacity = slots // shards
    brick_dev = vox_embed.shape[0]
    brick_size = vox_embed.shape[1]
    list_len = brick_tiles.shape[3]
    head_count = width // HD
    scale = 1.0 / HD**0.5
    group_size = min(brick_dev, max(1, 512 // brick_size))
    blocks = brick_dev // group_size
    tile_feats = cam_tiles[0]
    payload = (
        jnp.dot(tile_feats.reshape(-1, width), w_keyval, preferred_element_type=jnp.float32)
        .astype(jnp.bfloat16)
        .reshape(frames, tile_dev, pixels, 2 * width)
    )
    everything, all_plans = (
        lax.all_gather(payload, "brick", axis=1, tiled=True),
        lax.all_gather(tile_sends[0], "brick", axis=1, tiled=True),
    )
    own_plan = lax.dynamic_slice_in_dim(all_plans, own_index * capacity, capacity, 2)
    slot_index = (jnp.arange(shards, dtype=jnp.int32)[:, None] * tile_dev + own_plan).reshape(
        frames, slots
    )
    slot_data = jax.vmap(take_rows)(everything, slot_index)
    voxel_state = prev_state[0]
    behind = passed_along(voxel_state, "brick", 1)
    joined = jnp.concatenate([behind, voxel_state], 0)
    start = brick_dev - ego_shift[0, 0]
    shifted = lax.dynamic_slice_in_dim(joined, start, brick_dev, 0)
    q_in = vox_embed.astype(jnp.float32) + shifted.astype(jnp.float32)
    normed = rms_norm(q_in, norm_gains[0]).astype(jnp.bfloat16)
    queries = jnp.dot(
        normed.reshape(-1, width), w_query, preferred_element_type=jnp.float32
    ).astype(jnp.bfloat16)
    query_blocks = queries.reshape(blocks, group_size, brick_size, head_count, HD)
    keyval = slot_data[0]
    entries = brick_tiles[0, 0]

    def attend(operands):
        query_block, entry_block = operands
        gathered = keyval[jnp.maximum(entry_block, 0)].reshape(
            group_size, list_len * pixels, 2, head_count, HD
        )
        keys_part = gathered[:, :, 0]
        values_part = gathered[:, :, 1]
        scores = (
            jnp.einsum(
                "gqhd,gkhd->ghqk", query_block, keys_part, preferred_element_type=jnp.float32
            )
            * scale
        )
        live_keys = jnp.broadcast_to(
            (entry_block >= 0)[:, :, None], (group_size, list_len, pixels)
        ).reshape(group_size, 1, 1, list_len * pixels)
        scores = jnp.where(live_keys, scores, -1e30)
        row_peak = jnp.max(scores, axis=-1, keepdims=True)
        raised = jnp.exp(scores - row_peak)
        weights = (raised / jnp.sum(raised, axis=-1, keepdims=True)).astype(jnp.bfloat16)
        mixed = jnp.einsum(
            "ghqk,gkhd->gqhd", weights, values_part, preferred_element_type=jnp.float32
        )
        return mixed.astype(jnp.bfloat16)

    attended = lax.map(
        attend, (query_blocks, entries.reshape(blocks, group_size, list_len))
    ).reshape(-1, width)
    residual_x = q_in.reshape(-1, width) + jnp.dot(
        attended, w_attn_out, preferred_element_type=jnp.float32
    )
    hidden_in = rms_norm(residual_x, norm_gains[1]).astype(jnp.bfloat16)
    pre_act = jnp.dot(hidden_in, w_in, preferred_element_type=jnp.float32)
    activated = gelu_tanh(pre_act).astype(jnp.bfloat16)
    voxel_state = (
        (residual_x + jnp.dot(activated, w_out, preferred_element_type=jnp.float32))
        .astype(jnp.bfloat16)
        .reshape(brick_dev, brick_size, width)
    )
    cotangent = grad_out[0].reshape(-1, width)
    part_w_out = jnp.dot(activated.T, cotangent, preferred_element_type=jnp.float32)
    d_act = jnp.dot(cotangent, w_out.T, preferred_element_type=jnp.float32)
    unused_value, pullback = jax.vjp(gelu_tanh, pre_act)
    d_pre = pullback(d_act)[0].astype(jnp.bfloat16)
    part_w_in = jnp.dot(hidden_in.T, d_pre, preferred_element_type=jnp.float32)
    grad_w_in, grad_w_out = lax.psum((part_w_in, part_w_out), ("drive", "brick"))
    return (voxel_state[None], grad_w_in, grad_w_out)


def solution(mesh):
    return jax.shard_map(
        on_device,
        mesh=mesh,
        in_specs=(
            P("drive", None, "brick", None, None),
            P("brick", None, None),
            P("drive", "brick", None, None),
            P("drive", None, "brick", None),
            P("drive", None, "brick", None),
            P("drive", None),
            P(),
            P(),
            P(),
            P(),
            P(),
            P(),
            P("drive", "brick", None, None),
        ),
        out_specs=(P("drive", "brick", None, None), P(), P()),
        check_vma=False,
    )
```

profile of v0, /device:TPU:2, one launch (start us, length us, event | category | flops | bytes accessed | tf_op | source)
XLA Modules:
  0.0 652.4 jit_solution(17826369599442796199)
XLA Ops:
  11.9 58.8 %all-gather = s32[1,64,1,128]{3,2,0,1:T(1,128)S(1)} all-gather(s32[1,1,1,128]{3,2,0,1:T(1,128)} %bitcast.78), channel_id=2, replica_groups=mesh['drive'=4,'brick'=64] {'brick'}, dimensions={1}, use_global_device_ids=true | all-gather | bytes 33280 | tf_op jit(solution)/shard_map/all_gather | solution.py:66
  84.3 28.4 %all-gather.3.cloned.1.call-done = bf16[1,256,64,512]{3,2,0,1:T(8,128)(2,1)} async-done(((bf16[1,4,64,512]{3,2,0,1:T(8,128)(2,1)}), bf16[1,256,64,512]{3,2,0,1:T(8,128)(2,1)}) %all-gather.3.cloned.1.call-update) | async-done | bytes 16777232 | tf_op jit(solution)/shard_map/all_gather | solution.py:65
  112.7 12.5 %gather_fusion.1 = bf16[128,64,512]{2,1,0:T(8,128)(2,1)} fusion(bf16[1,256,64,512]{3,2,0,1:T(8,128)(2,1)} %all-gather.3.cloned.1.call-done, s32[128]{0:T(128)S(1)} %or_bitcast_fusion), kind=kCustom, calls=%fused_computation.1 | custom fusion | bytes 16778240 | tf_op jit(solution)/shard_map/vmap()/gather | solution.py:25
  125.2 235.8 %while.10 = (s32[]{:T(128)}, bf16[6,4,128,8,32]{2,1,0,4,3:T(4,128)(2,1)}, s32[6,4,8]{2,1,0:T(4,128)S(1)}, bf16[128,64,512]{2,1,0:T(8,128)(2,1)}, bf16[6,4,128,8,32]{2,1,0,4,3:T(4,128)(2,1)}, /*index=5*/s32[]{:T(128)}) while((s32[]{:T(128)}, bf16[6,4,128,8,32]{2,1,0,4,3:T(4,128)(2,1)}, s32[6,4,8]{2,1,0:T(4,128)S(1)}, ...), condition=%wide.region_4.5_spmd, body=%wide.region_1.4_spmd.sunk | while | flops 285345344 | bytes 54048272 | solution.py:112
  130.6 7.4 %copy.61 = bf16[32,64,512]{1,0,2:T(8,128)(2,1)} copy(bf16[32,64,512]{2,1,0:T(8,128)(2,1)} %gather_fusion) | data formatting | bytes 4194304 | tf_op jit(solution)/shard_map/while/body/eval_jaxpr/gather | solution.py:89
  138.1 6.7 %reshape.153 = bf16[4,512,2,8,32]{1,0,4,3,2:T(4,128)(2,1)} reshape(bf16[32,64,512]{1,0,2:T(8,128)(2,1)} %copy.61) | data formatting | bytes 4194304 | tf_op jit(solution)/shard_map/while/body/eval_jaxpr/reshape | solution.py:89
  152.8 8.7 %fusion.54 = (f32[4,8,128]{2,1,0:T(8,128)S(1)}, f32[4,8,128,512]{3,2,1,0:T(8,128)S(1)}) fusion(f32[4,8,128,512]{3,2,1,0:T(8,128)} %fusion.53, pred[4,512]{1,0:T(4,128)(4,1)S(1)} %broadcast_in_dim.57), kind=kOutput, calls=%fused_computation.65.clone.1 | output fusion | flops 12583423 | bytes 16795648 | tf_op jit(solution)/shard_map/while/body/eval_jaxpr/sub | solution.py:105
  169.9 7.4 %copy.61 = bf16[32,64,512]{1,0,2:T(8,128)(2,1)} copy(bf16[32,64,512]{2,1,0:T(8,128)(2,1)} %gather_fusion) | data formatting | bytes 4194304 | tf_op jit(solution)/shard_map/while/body/eval_jaxpr/gather | solution.py:89
  177.3 6.7 %reshape.153 = bf16[4,512,2,8,32]{1,0,4,3,2:T(4,128)(2,1)} reshape(bf16[32,64,512]{1,0,2:T(8,128)(2,1)} %copy.61) | data formatting | bytes 4194304 | tf_op jit(solution)/shard_map/while/body/eval_jaxpr/reshape | solution.py:89
  192.1 8.7 %fusion.54 = (f32[4,8,128]{2,1,0:T(8,128)S(1)}, f32[4,8,128,512]{3,2,1,0:T(8,128)S(1)}) fusion(f32[4,8,128,512]{3,2,1,0:T(8,128)} %fusion.53, pred[4,512]{1,0:T(4,128)(4,1)S(1)} %broadcast_in_dim.57), kind=kOutput, calls=%fused_computation.65.clone.1 | output fusion | flops 12583423 | bytes 16795648 | tf_op jit(solution)/shard_map/while/body/eval_jaxpr/sub | solution.py:105
  209.2 7.4 %copy.61 = bf16[32,64,512]{1,0,2:T(8,128)(2,1)} copy(bf16[32,64,512]{2,1,0:T(8,128)(2,1)} %gather_fusion) | data formatting | bytes 4194304 | tf_op jit(solution)/shard_map/while/body/eval_jaxpr/gather | solution.py:89
  216.6 6.7 %reshape.153 = bf16[4,512,2,8,32]{1,0,4,3,2:T(4,128)(2,1)} reshape(bf16[32,64,512]{1,0,2:T(8,128)(2,1)} %copy.61) | data formatting | bytes 4194304 | tf_op jit(solution)/shard_map/while/body/eval_jaxpr/reshape | solution.py:89
  231.4 8.7 %fusion.54 = (f32[4,8,128]{2,1,0:T(8,128)S(1)}, f32[4,8,128,512]{3,2,1,0:T(8,128)S(1)}) fusion(f32[4,8,128,512]{3,2,1,0:T(8,128)} %fusion.53, pred[4,512]{1,0:T(4,128)(4,1)S(1)} %broadcast_in_dim.57), kind=kOutput, calls=%fused_computation.65.clone.1 | output fusion | flops 12583423 | bytes 16795648 | tf_op jit(solution)/shard_map/while/body/eval_jaxpr/sub | solution.py:105
  248.5 7.4 %copy.61 = bf16[32,64,512]{1,0,2:T(8,128)(2,1)} copy(bf16[32,64,512]{2,1,0:T(8,128)(2,1)} %gather_fusion) | data formatting | bytes 4194304 | tf_op jit(solution)/shard_map/while/body/eval_jaxpr/gather | solution.py:89
  255.9 6.7 %reshape.153 = bf16[4,512,2,8,32]{1,0,4,3,2:T(4,128)(2,1)} reshape(bf16[32,64,512]{1,0,2:T(8,128)(2,1)} %copy.61) | data formatting | bytes 4194304 | tf_op jit(solution)/shard_map/while/body/eval_jaxpr/reshape | solution.py:89
  270.7 8.7 %fusion.54 = (f32[4,8,128]{2,1,0:T(8,128)S(1)}, f32[4,8,128,512]{3,2,1,0:T(8,128)S(1)}) fusion(f32[4,8,128,512]{3,2,1,0:T(8,128)} %fusion.53, pred[4,512]{1,0:T(4,128)(4,1)S(1)} %broadcast_in_dim.57), kind=kOutput, calls=%fused_computation.65.clone.1 | output fusion | flops 12583423 | bytes 16795648 | tf_op jit(solution)/shard_map/while/body/eval_jaxpr/sub | solution.py:105
  287.8 7.4 %copy.61 = bf16[32,64,512]{1,0,2:T(8,128)(2,1)} copy(bf16[32,64,512]{2,1,0:T(8,128)(2,1)} %gather_fusion) | data formatting | bytes 4194304 | tf_op jit(solution)/shard_map/while/body/eval_jaxpr/gather | solution.py:89
  295.2 6.7 %reshape.153 = bf16[4,512,2,8,32]{1,0,4,3,2:T(4,128)(2,1)} reshape(bf16[32,64,512]{1,0,2:T(8,128)(2,1)} %copy.61) | data formatting | bytes 4194304 | tf_op jit(solution)/shard_map/while/body/eval_jaxpr/reshape | solution.py:89
  310.0 8.7 %fusion.54 = (f32[4,8,128]{2,1,0:T(8,128)S(1)}, f32[4,8,128,512]{3,2,1,0:T(8,128)S(1)}) fusion(f32[4,8,128,512]{3,2,1,0:T(8,128)} %fusion.53, pred[4,512]{1,0:T(4,128)(4,1)S(1)} %broadcast_in_dim.57), kind=kOutput, calls=%fused_computation.65.clone.1 | output fusion | flops 12583423 | bytes 16795648 | tf_op jit(solution)/shard_map/while/body/eval_jaxpr/sub | solution.py:105
  327.1 7.4 %copy.61 = bf16[32,64,512]{1,0,2:T(8,128)(2,1)} copy(bf16[32,64,512]{2,1,0:T(8,128)(2,1)} %gather_fusion) | data formatting | bytes 4194304 | tf_op jit(solution)/shard_map/while/body/eval_jaxpr/gather | solution.py:89
  334.5 6.7 %reshape.153 = bf16[4,512,2,8,32]{1,0,4,3,2:T(4,128)(2,1)} reshape(bf16[32,64,512]{1,0,2:T(8,128)(2,1)} %copy.61) | data formatting | bytes 4194304 | tf_op jit(solution)/shard_map/while/body/eval_jaxpr/reshape | solution.py:89
  349.3 8.7 %fusion.54 = (f32[4,8,128]{2,1,0:T(8,128)S(1)}, f32[4,8,128,512]{3,2,1,0:T(8,128)S(1)}) fusion(f32[4,8,128,512]{3,2,1,0:T(8,128)} %fusion.53, pred[4,512]{1,0:T(4,128)(4,1)S(1)} %broadcast_in_dim.57), kind=kOutput, calls=%fused_computation.65.clone.1 | output fusion | flops 12583423 | bytes 16795648 | tf_op jit(solution)/shard_map/while/body/eval_jaxpr/sub | solution.py:105
  374.7 9.6 %fusion.19 = f32[256,512]{1,0:T(8,128)} fusion(f32[3072,512]{1,0:T(8,128)} %get-tuple-element.69, bf16[3072,256]{1,0:T(8,128)(2,1)S(1)} %bitcast.65, bf16[512,256]{1,0:T(8,128)(2,1)S(1)} %copy-done.4, f32[3072,256]{1,0:T(8,128)} %copy-done.2, f32[256]{0:T(256)S(1)} %bitcast.77, f32[3072]{0:T(1024)S(1)} %add_rsqrt_fusion), kind=kOutput, calls=%fused_computation.45 | convolution fusion | flops 1644429312 | bytes 11809792 | tf_op jit(solution)/shard_map/dot_general | solution.py:131
  389.3 252.5 %all-reduce.3.cloned.1.call-done = (f32[256,512]{1,0:T(8,128)}, f32[512,256]{1,0:T(8,128)}) async-done(((f32[256,512]{1,0:T(8,128)}, f32[512,256]{1,0:T(8,128)}), (f32[256,512]{1,0:T(8,128)}, f32[512,256]{1,0:T(8,128)})) %all-reduce.3.cloned.1.call-update) | async-done | bytes 1048592 | tf_op jit(solution)/shard_map/psum | solution.py:132
  (121 shorter events, 138.3 us)
Async XLA Ops:
  7.2 364.0 %copy-start = (bf16[1,24,128,256]{3,2,1,0:T(8,128)(2,1)S(1)}, bf16[1,24,128,256]{3,2,1,0:T(8,128)(2,1)}, u32[]{:S(2)}) copy-start(bf16[1,24,128,256]{3,2,1,0:T(8,128)(2,1)} %param.27) | copy-start | bytes 4718596
  7.2 105.5 %all-gather.3.cloned.1.call-start = ((), (), s32[]{:S(2)}) async-start(), calls=%async_computation | async-start | bytes 17039360 | tf_op jit(solution)/shard_map/all_gather | solution.py:65
  9.3 632.6 %all-reduce.3.cloned.1.call-start = ((), (), s32[]{:S(2)}) async-start(), calls=%async_computation.1 | async-start | bytes 2097152 | tf_op jit(solution)/shard_map/psum | solution.py:132
  9.3 63.4 %collective-permute-start = (bf16[24,128,256]{2,1,0:T(8,128)(2,1)}, bf16[24,128,256]{2,1,0:T(8,128)(2,1)S(1)}, u32[]{:S(2)}, u32[]{:S(2)}) collective-permute-start(bf16[24,128,256]{2,1,0:T(8,128)(2,1)} %bitcast.70), channel_id=1, source_target_pairs={{0,1},{1,2},{2,3},{3,4},{4,5},{5,6},{6,7},{7,8},{8,9},{9,10},{10,1... | collective-permute-start | bytes 4718600 | tf_op jit(solution)/shard_map/ppermute | solution.py:12
  75.3 1.7 copy-start.1
  75.3 2.2 copy-start.6
  360.9 2.9 copy-start.5
  363.8 3.1 copy-start.7
  366.8 4.4 copy-start.2
  371.2 1.7 copy-start.3
  371.2 3.5 copy-start.4
Sparse Core Ops, SparseCore 0:
  11.3 101.2 all-gather.2
  384.5 257.3 all-reduce.2
where the time goes:
time: 655 us; the launch traced here: 652 us
  waiting for transfers between devices  281 us (43%)
  local copies, waits for them, and re-layouts  175 us (27%)
  matrix products  65.4 us (10%)
  blocking collectives  58.8 us (9%)
  other arithmetic  55.6 us (8%)
  between operations  14.8 us (2%)
    psum x1, waiting for transfers between devices, on_device(): lax.psum((part_w_in, part_w_out), ('drive', 'brick'))  253 us
    gather x12, local copies, waits for them, and re-layouts, attend(): keyval[jnp.maximum(entry_block, 0)]  76.8 us
    all_gather x1, blocking collectives, on_device(): lax.all_gather(tile_sends[0], 'brick', axis=1, tiled=True)  58.8 us
    sub x6, other arithmetic, attend(): raised = jnp.exp(scores - row_peak)  52.4 us
    reshape x6, local copies, waits for them, and re-layouts, attend(): keyval[jnp.maximum(entry_block, 0)]  40.4 us
    all_gather x1, waiting for transfers between devices, on_device(): lax.all_gather(payload, 'brick', axis=1, tiled=True)  28.4 us
    dot_general x6, matrix products, attend(): jnp.einsum('gqhd,gkhd->ghqk', query_block, keys_part, preferred_element_t...  27.2 us
    slice x6, local copies, waits for them, and re-layouts, attend(): values_part = gathered[:, :, 1]  13.6 us
  transfers between devices with their start and end apart: 3, of which 2 were waited for; matrix products, arithmetic and copies ran while one was open for 3% of the time, Pallas kernels for 0%

commit v1 on v0

v1 whole, which is shorter than its diff:
```python
import functools

import jax
import jax.numpy as jnp
from jax import lax
from jax.experimental import pallas as pl
from jax.experimental.pallas import tpu as pltpu
from jax.sharding import PartitionSpec as P

HD = 32
GROUP = 4
NT = (((1,), (1,)), ((), ()))
TN = (((0,), (0,)), ((), ()))


def dot(a, b, dims=(((1,), (0,)), ((), ()))):
    return lax.dot_general(a, b, dims, preferred_element_type=jnp.float32)


def rms_norm(values, norm_gain):
    mean_sq = jnp.mean(values * values, axis=-1, keepdims=True)
    return values * lax.rsqrt(mean_sq + 1e-06) * norm_gain


def step_kernel(
    sends,
    entries,
    shift,
    cams,
    behind,
    prev,
    vox,
    cot,
    gains,
    w_query,
    w_key,
    w_value_t,
    w_attn_out,
    w_in,
    w_out,
    new_state,
    grad_in,
    grad_out,
    qin_s,
    query_s,
    att_s,
    feat_s,
):
    step = pl.program_id(0)
    bricks = prev.shape[0]
    size = prev.shape[1]
    width = prev.shape[2]
    list_len = entries.shape[0] // bricks
    pixels = cams.shape[1]
    tile_dev = cams.shape[0] // (sends.shape[0] // 2)
    rows = GROUP * size
    log2_scale = 1.4426950408889634 / HD**0.5

    @pl.when(step == 0)
    def _():
        grad_in[...] = jnp.zeros_like(grad_in)
        grad_out[...] = jnp.zeros_like(grad_out)
        feat_s[...] = jnp.zeros_like(feat_s)

    start = bricks - shift[0]
    for g in range(GROUP):
        at = start + step * GROUP + g
        from_behind = behind[jnp.minimum(at, bricks - 1)].astype(jnp.float32)
        from_own = prev[jnp.maximum(at - bricks, 0)].astype(jnp.float32)
        shifted = jnp.where(at < bricks, from_behind, from_own)
        q_in = vox[g].astype(jnp.float32) + shifted
        here = pl.ds(g * size, size)
        qin_s[here, :] = q_in
        normed = rms_norm(q_in, gains[0:1, :]).astype(jnp.bfloat16)
        query_s[here, :] = dot(normed, w_query[...]).astype(jnp.bfloat16)

    lane_head = lax.broadcasted_iota(jnp.int32, (size, width), 1) // HD

    def one_brick(g, carry):
        brick = step * GROUP + g
        live = jnp.int32(0)
        for e in range(list_len):
            entry = entries[brick * list_len + e]

            @pl.when(entry >= 0)
            def _(entry=entry, live=live):
                tile = (entry // 2) * tile_dev + sends[entry]
                feat_s[pl.ds(pl.multiple_of(live * pixels, pixels), pixels), :] = cams[tile]

            live = live + (entry >= 0).astype(jnp.int32)
        here = pl.ds(pl.multiple_of(g * size, size), size)
        pair_count = (live + 1) // 2
        cap = jnp.where(live % 2 == 1, jnp.float32(-1e30), jnp.float32(3e38))
        for pairs in range(1, list_len // 2 + 1):

            @pl.when(pair_count == pairs)
            def _(pairs=pairs):
                n = pairs * 2 * pixels
                feats = feat_s[0:n, :]
                keys = dot(feats, w_key[...]).astype(jnp.bfloat16)
                values_t = dot(w_value_t[...], feats, NT).astype(jnp.bfloat16)
                query = query_s[here, :]
                outs = []
                for hp in range(width // HD // 2):
                    masked = [
                        jnp.where(lane_head == h, query, jnp.zeros_like(query))
                        for h in (2 * hp, 2 * hp + 1)
                    ]
                    scores = dot(keys, jnp.concatenate(masked, 0), NT)
                    scores = jnp.concatenate(
                        [scores[: n - pixels], jnp.minimum(scores[n - pixels :], cap)], 0
                    )
                    peak = jnp.max(scores, axis=0, keepdims=True)
                    raised = jnp.exp2((scores - peak) * log2_scale)
                    inverse = 1.0 / jnp.sum(raised, axis=0, keepdims=True)
                    weights = (raised * inverse).astype(jnp.bfloat16)
                    mixed = dot(values_t[2 * HD * hp : 2 * HD * (hp + 1), :], weights)
                    outs.append(mixed[:HD, :size])
                    outs.append(mixed[HD:, size:])
                att_s[here, :] = jnp.concatenate(outs, 0).T.astype(jnp.bfloat16)

        return carry

    lax.fori_loop(0, GROUP, one_brick, 0)

    residual = qin_s[...] + dot(att_s[...], w_attn_out[...])
    hidden = rms_norm(residual, gains[1:2, :]).astype(jnp.bfloat16)
    pre = dot(hidden, w_in[...])
    square = pre * pre
    root = 0.7978845608028654
    tanh = jnp.tanh(root * (pre + 0.044715 * (square * pre)))
    half = 0.5 * (1.0 + tanh)
    act = (pre * half).astype(jnp.bfloat16)
    new_state[...] = (
        (residual + dot(act, w_out[...])).astype(jnp.bfloat16).reshape(GROUP, size, width)
    )
    cotangent = cot[...].reshape(rows, width)
    d_act = dot(cotangent, w_out[...], NT)
    slope = half + (0.5 * root) * pre * (1.0 - tanh * tanh) * (1.0 + (3 * 0.044715) * square)
    d_pre = (d_act * slope).astype(jnp.bfloat16)
    grad_out[...] += dot(act, cotangent, TN)
    grad_in[...] += dot(hidden, d_pre, TN)


def local_step(
    sends, entries, shift, cams, behind, prev, vox, cot, gains, w_query, w_keyval, w_attn_out,
    w_in, w_out, interpret=False,
):
    bricks, size, width = prev.shape
    hidden = w_in.shape[1]
    rows = GROUP * size
    list_len = entries.shape[0] // bricks

    def whole(array):
        zeros = (0,) * array.ndim
        return pl.BlockSpec(array.shape, lambda i, *_: zeros, pipeline_mode=pl.Buffered(1))

    block = pl.BlockSpec((GROUP, size, width), lambda i, *_: (i, 0, 0))
    operands = (
        cams,
        behind,
        prev,
        vox,
        cot,
        gains,
        w_query,
        w_keyval[:, :width],
        w_keyval[:, width:].T,
        w_attn_out,
        w_in,
        w_out,
    )
    specs = [block if a is vox or a is cot else whole(a) for a in operands]
    return pl.pallas_call(
        step_kernel,
        out_shape=(
            jax.ShapeDtypeStruct((bricks, size, width), jnp.bfloat16),
            jax.ShapeDtypeStruct((width, hidden), jnp.float32),
            jax.ShapeDtypeStruct((hidden, width), jnp.float32),
        ),
        grid_spec=pltpu.PrefetchScalarGridSpec(
            num_scalar_prefetch=3,
            grid=(bricks // GROUP,),
            in_specs=specs,
            out_specs=(
                block,
                pl.BlockSpec((width, hidden), lambda i, *_: (0, 0)),
                pl.BlockSpec((hidden, width), lambda i, *_: (0, 0)),
            ),
            scratch_shapes=[
                pltpu.VMEM((rows, width), jnp.float32),
                pltpu.VMEM((rows, width), jnp.bfloat16),
                pltpu.VMEM((rows, width), jnp.bfloat16),
                pltpu.VMEM((list_len * cams.shape[1], width), jnp.bfloat16),
            ],
        ),
        compiler_params=pltpu.CompilerParams(vmem_limit_bytes=48 << 20),
        name="voxel_step",
        interpret=interpret,
    )(sends, entries, shift, *operands)


def on_device(
    cam_tiles,
    vox_embed,
    prev_state,
    tile_sends,
    brick_tiles,
    ego_shift,
    norm_gains,
    w_query,
    w_keyval,
    w_attn_out,
    w_in,
    w_out,
    grad_out,
):
    shards = lax.axis_size("brick")
    prev = prev_state[0]
    cams = lax.all_gather(cam_tiles[0, 0], "brick", axis=0, tiled=True)
    own_plan = lax.all_to_all(
        tile_sends[0, 0].reshape(shards, -1), "brick", 0, 0, tiled=True
    ).reshape(-1)
    behind = lax.ppermute(prev, "brick", [(i, i + 1) for i in range(shards - 1)])
    new_state, grad_w_in, grad_w_out = local_step(
        own_plan,
        brick_tiles[0, 0].reshape(-1),
        ego_shift[0],
        cams,
        behind,
        prev,
        vox_embed,
        grad_out[0],
        norm_gains,
        w_query,
        w_keyval,
        w_attn_out,
        w_in,
        w_out,
    )
    grad_w_in, grad_w_out = lax.psum((grad_w_in, grad_w_out), ("drive", "brick"))
    return (new_state[None], grad_w_in, grad_w_out)


def solution(mesh):
    return jax.shard_map(
        on_device,
        mesh=mesh,
        in_specs=(
            P("drive", None, "brick", None, None),
            P("brick", None, None),
            P("drive", "brick", None, None),
            P("drive", None, "brick", None),
            P("drive", None, "brick", None),
            P("drive", None),
            P(),
            P(),
            P(),
            P(),
            P(),
            P(),
            P("drive", "brick", None, None),
        ),
        out_specs=(P("drive", "brick", None, None), P(), P()),
        check_vma=False,
    )
```

time: 655 us -> 426 us (0.65)
  local copies, waits for them, and re-layouts: 175 us -> 12.9 us
  matrix products: 65.4 us -> 0 us
  blocking collectives: 58.8 us -> 0 us
  other arithmetic: 55.6 us -> 2.04 us
  waiting for transfers between devices: 281 us -> 331 us
  Pallas kernels: 0 us -> 49.9 us
  starting transfers between devices: 2 us -> 14.8 us
    gather x14 -> x0, local copies, waits for them, and re-layouts: 89.3 us -> none  [the longest x12 76.8 us: attend(): keyval[jnp.maximum(entry_block, 0)]]
    dot_general x19 -> x0, matrix products: 65.4 us -> none  [the longest x6 27.2 us: attend(): jnp.einsum('gqhd,gkhd->ghqk', query_block, keys_part, preferred_element_t...]
    all_gather x1 -> x0, blocking collectives: 58.8 us -> none  [on_device(): lax.all_gather(tile_sends[0], 'brick', axis=1, tiled=True)]
    sub x6 -> x0, other arithmetic: 52.4 us -> none  [attend(): raised = jnp.exp(scores - row_peak)]
    pallas_call x0 -> x1, Pallas kernels: none -> 49.9 us  [local_step(): pl.pallas_call(step_kernel, out_shape=(jax.ShapeDtypeStruct((bricks, size...]
    reshape x9 -> x1, local copies, waits for them, and re-layouts: 47.6 us -> 0.13 us  [on_device(): own_plan = lax.all_to_all(tile_sends[0, 0].reshape(shards, -1), 'brick',...]
    all_gather x1, waiting for transfers between devices: 28.4 us -> 55.1 us  [on_device(): cams = lax.all_gather(cam_tiles[0, 0], 'brick', axis=0, tiled=True)]
    slice x7 -> x1, local copies, waits for them, and re-layouts: 14.3 us -> 1 us  [local_step(): w_keyval[:, width:]]
  transfers between devices with their start and end apart: 3 -> 4, of which waited for: 2 -> 3; matrix products, arithmetic and copies ran while one was open for 3% -> 1% of each run, Pallas kernels for 0% -> 0%
where the time goes in v1:
time: 426 us; the launch traced here: 425 us
  waiting for transfers between devices  331 us (78%)
  Pallas kernels  49.9 us (12%)
  starting transfers between devices  14.8 us (3%)
  between operations  14.7 us (3%)
  local copies, waits for them, and re-layouts  12.9 us (3%)
    psum x1, waiting for transfers between devices, on_device(): lax.psum((grad_w_in, grad_w_out), ('drive', 'brick'))  263 us
    all_gather x1, waiting for transfers between devices, on_device(): cams = lax.all_gather(cam_tiles[0, 0], 'brick', axis=0, tiled=True)  55.1 us
    pallas_call x1, Pallas kernels, local_step(): pl.pallas_call(step_kernel, out_shape=(jax.ShapeDtypeStruct((bricks, size...  49.9 us
    all_to_all x1, starting transfers between devices, on_device(): lax.all_to_all(tile_sends[0, 0].reshape(shards, -1), 'brick', 0, 0, tiled...  12.7 us
    all_to_all x1, waiting for transfers between devices, on_device(): lax.all_to_all(tile_sends[0, 0].reshape(shards, -1), 'brick', 0, 0, tiled...  11.7 us
    unnamed x17, local copies, waits for them, and re-layouts  10.9 us
  transfers between devices with their start and end apart: 4, of which 3 were waited for; matrix products, arithmetic and copies ran while one was open for 1% of the time, Pallas kernels for 0%

profile of v1, /device:TPU:2, one launch (start us, length us, event | category | flops | bytes accessed | tf_op | source)
XLA Modules:
  0.0 424.9 jit_solution(6056932971211039325)
XLA Ops:
  7.2 0.7 all-gather.3.cloned.1.call-update
  7.9 1.9 collective-permute-start
  9.8 0.5 broadcast.6
  10.3 1.3 reduce.6
  11.7 0.8 all_to_all.6
  12.4 12.7 %all-to-all-start = ((s32[64,1,2]{2,1,0:T(1,128)}), s32[64,1,2]{2,1,0:T(1,128)S(1)}, u32[]{:S(2)}, u32[]{:S(2)}) async-start(s32[64,1,2]{2,1,0:T(1,128)} %bitcast), calls=%async_computation | async-start | bytes 65536 | tf_op jit(solution)/shard_map/all_to_all | solution.py:221
  25.2 1.0 fusion
  26.9 0.8 copy.20
  27.6 0.1 reshape_squeeze.4.entries
  27.7 0.1 copy.23
  27.8 11.7 %all-to-all-done = s32[64,1,2]{2,1,0:T(1,128)S(1)} async-done(((s32[64,1,2]{2,1,0:T(1,128)}), s32[64,1,2]{2,1,0:T(1,128)S(1)}, u32[]{:S(2)}, u32[]{:S(2)}) %all-to-all-start) | async-done | bytes 544 | tf_op jit(solution)/shard_map/all_to_all | solution.py:221
  39.5 0.7 reduce.7
  40.2 0.1 reshape.13.sends
  40.4 55.1 %all-gather.3.cloned.1.call-done = bf16[1,1,256,64,256]{4,3,1,0,2:T(8,128)(2,1)} async-done(((bf16[1,1,4,64,256]{4,3,1,0,2:T(8,128)(2,1)}), bf16[1,1,256,64,256]{4,3,1,0,2:T(8,128)(2,1)}) %all-gather.3.cloned.1.call-update) | async-done | bytes 8388624 | tf_op jit(solution)/shard_map/all_gather | solution.py:220
  95.5 1.4 copy-done
  96.9 0.9 copy-done.1
  97.8 0.9 copy-done.2
  98.8 0.9 copy-done.3
  99.7 0.9 copy-done.4
  100.6 0.7 copy-done.5
  101.3 49.9 %voxel_step.1 = (bf16[24,128,256]{2,1,0:T(8,128)(2,1)}, f32[256,512]{1,0:T(8,128)}, f32[512,256]{1,0:T(8,128)}) custom-call(s32[128]{0:T(128)S(1)} %reshape.13.sends, s32[192]{0:T(256)S(1)} %reshape_squeeze.4.entries, s32[1]{0:T(128)} %bitcast.10.shift, bf16[256,64,256]{2,1,0:T(8,128)(2,1)} %bitcast.14, ...), custom_call_target="tpu_custom_call" | custom-call | tf_op jit(solution)/shard_map/voxel_step/pallas_call | solution.py:174
  151.2 263.1 %all-reduce.3.cloned.1.call-done = (f32[256,512]{1,0:T(8,128)}, f32[512,256]{1,0:T(8,128)}) async-done(((f32[256,512]{1,0:T(8,128)}, f32[512,256]{1,0:T(8,128)}), (f32[256,512]{1,0:T(8,128)}, f32[512,256]{1,0:T(8,128)})) %all-reduce.3.cloned.1.call-update) | async-done | bytes 1048592 | tf_op jit(solution)/shard_map/psum | solution.py:241
  414.4 1.9 copy.27
  416.2 1.9 copy.28
  (10 shorter events, 0.1 us)
Async XLA Ops:
  7.2 88.3 %all-gather.3.cloned.1.call-start = ((), (), s32[]{:S(2)}) async-start(), calls=%async_computation.1 | async-start | bytes 8519680 | tf_op jit(solution)/shard_map/all_gather | solution.py:220
  7.9 32.5 %collective-permute-start = (bf16[24,128,256]{2,1,0:T(8,128)(2,1)}, bf16[24,128,256]{2,1,0:T(8,128)(2,1)S(1)}, u32[]{:S(2)}, u32[]{:S(2)}) collective-permute-start(bf16[24,128,256]{2,1,0:T(8,128)(2,1)} %bitcast.11), channel_id=1, source_target_pairs={{0,1},{1,2},{2,3},{3,4},{4,5},{5,6},{6,7},{7,8},{8,9},{9,10},{10,1... | collective-permute-start | bytes 4718600 | tf_op jit(solution)/shard_map/ppermute | solution.py:224
  12.4 27.1 %all-to-all-start = ((s32[64,1,2]{2,1,0:T(1,128)}), s32[64,1,2]{2,1,0:T(1,128)S(1)}, u32[]{:S(2)}, u32[]{:S(2)}) async-start(s32[64,1,2]{2,1,0:T(1,128)} %bitcast), calls=%async_computation | async-start | bytes 65536 | tf_op jit(solution)/shard_map/all_to_all | solution.py:221
  25.2 389.2 %all-reduce.3.cloned.1.call-start = ((), (), s32[]{:S(2)}) async-start(), calls=%async_computation.2 | async-start | bytes 2097152 | tf_op jit(solution)/shard_map/psum | solution.py:241
  95.5 1.4 copy-start
  96.9 0.9 copy-start.1
  97.8 0.9 copy-start.2
  98.8 0.9 copy-start.3
  99.7 0.9 copy-start.4
  100.6 0.7 copy-start.5
Sparse Core Ops, SparseCore 0:
  10.7 84.6 all-gather.2
  151.4 262.9 all-reduce.2

commit v2 on v1

--- a/solution.py
+++ b/solution.py
@@ -39,8 +39,7 @@
     w_in,
     w_out,
     new_state,
-    grad_in,
-    grad_out,
+    grads,
     qin_s,
     query_s,
     att_s,
@@ -58,8 +57,7 @@
 
     @pl.when(step == 0)
     def _():
-        grad_in[...] = jnp.zeros_like(grad_in)
-        grad_out[...] = jnp.zeros_like(grad_out)
+        grads[...] = jnp.zeros_like(grads)
         feat_s[...] = jnp.zeros_like(feat_s)
 
     start = bricks - shift[0]
@@ -138,8 +136,10 @@
     d_act = dot(cotangent, w_out[...], NT)
     slope = half + (0.5 * root) * pre * (1.0 - tanh * tanh) * (1.0 + (3 * 0.044715) * square)
     d_pre = (d_act * slope).astype(jnp.bfloat16)
-    grad_out[...] += dot(act, cotangent, TN)
-    grad_in[...] += dot(hidden, d_pre, TN)
+    ff = act.shape[1]
+    grads[:ff, :] += dot(act, cotangent, TN)
+    grads[ff : ff + width, :] += dot(hidden, d_pre[:, :width], TN)
+    grads[ff + width :, :] += dot(hidden, d_pre[:, width:], TN)
 
 
 def local_step(
@@ -175,8 +175,7 @@
         step_kernel,
         out_shape=(
             jax.ShapeDtypeStruct((bricks, size, width), jnp.bfloat16),
-            jax.ShapeDtypeStruct((width, hidden), jnp.float32),
-            jax.ShapeDtypeStruct((hidden, width), jnp.float32),
+            jax.ShapeDtypeStruct((2 * hidden, width), jnp.float32),
         ),
         grid_spec=pltpu.PrefetchScalarGridSpec(
             num_scalar_prefetch=3,
@@ -184,8 +183,7 @@
             in_specs=specs,
             out_specs=(
                 block,
-                pl.BlockSpec((width, hidden), lambda i, *_: (0, 0)),
-                pl.BlockSpec((hidden, width), lambda i, *_: (0, 0)),
+                pl.BlockSpec((2 * hidden, width), lambda i, *_: (0, 0)),
             ),
             scratch_shapes=[
                 pltpu.VMEM((rows, width), jnp.float32),
@@ -198,6 +196,40 @@
         name="voxel_step",
         interpret=interpret,
     )(sends, entries, shift, *operands)
+
+
+SCATTER = ((1, 1), (16, 48), (48, 32), (2, 2), (4, 12))
+WHOLE = (("brick", 12), ("drive", 1), ("drive", 3))
+
+
+def swapped(value, axis, mask):
+    pairs = [(i, i ^ mask) for i in range(lax.axis_size(axis))]
+    return lax.ppermute(value, axis, pairs)
+
+
+def parity(index, bits):
+    return sum((index // (1 << k)) % 2 for k in range(6) if bits >> k & 1) % 2
+
+
+def sum_over_devices(value):
+    me = lax.axis_index("brick")
+    for mask, bits in SCATTER:
+        rows = value.shape[0] // 2
+        side = parity(me, bits)
+        kept = lax.dynamic_slice_in_dim(value, side * rows, rows, 0)
+        sent = lax.dynamic_slice_in_dim(value, (1 - side) * rows, rows, 0)
+        value = kept + swapped(sent, "brick", mask)
+    for axis, mask in WHOLE:
+        value = value + swapped(value, axis, mask)
+    for mask, bits in reversed(SCATTER):
+        other = swapped(value, "brick", mask)
+        first = parity(me, bits) == 0
+        value = jnp.where(
+            first,
+            jnp.concatenate([value, other], 0),
+            jnp.concatenate([other, value], 0),
+        )
+    return value
 
 
 def on_device(
@@ -222,7 +254,7 @@
         tile_sends[0, 0].reshape(shards, -1), "brick", 0, 0, tiled=True
     ).reshape(-1)
     behind = lax.ppermute(prev, "brick", [(i, i + 1) for i in range(shards - 1)])
-    new_state, grad_w_in, grad_w_out = local_step(
+    new_state, grads = local_step(
         own_plan,
         brick_tiles[0, 0].reshape(-1),
         ego_shift[0],
@@ -238,7 +270,10 @@
         w_in,
         w_out,
     )
-    grad_w_in, grad_w_out = lax.psum((grad_w_in, grad_w_out), ("drive", "brick"))
+    total = sum_over_devices(grads)
+    width, hidden = w_in.shape
+    grad_w_out = total[:hidden]
+    grad_w_in = jnp.concatenate([total[hidden : hidden + width], total[hidden + width :]], 1)
     return (new_state[None], grad_w_in, grad_w_out)
 
 

time: 426 us -> 232 us (0.54)
  waiting for transfers between devices: 331 us -> 108 us
  starting transfers between devices: 14.8 us -> 42.8 us
    psum x1 -> x0, waiting for transfers between devices: 263 us -> none  [on_device(): lax.psum((grad_w_in, grad_w_out), ('drive', 'brick'))]
    ppermute x0 -> x13, waiting for transfers between devices: none -> 40.2 us  [swapped(): return lax.ppermute(value, axis, pairs)]
    ppermute x0 -> x13, starting transfers between devices: none -> 28.1 us  [swapped(): return lax.ppermute(value, axis, pairs)]
    unnamed x17 -> x15, local copies, waits for them, and re-layouts: 10.9 us -> 7.17 us
  transfers between devices with their start and end apart: 4 -> 16, of which waited for: 3 -> 15; matrix products, arithmetic and copies ran while one was open for 1% -> 2% of each run, Pallas kernels for 0% -> 0%
where the time goes in v2:
time: 232 us; the launch traced here: 230 us
  waiting for transfers between devices  108 us (47%)
  Pallas kernels  50.8 us (22%)
  starting transfers between devices  42.8 us (18%)
  between operations  14.9 us (6%)
  local copies, waits for them, and re-layouts  10.1 us (4%)
  other arithmetic  3.2 us (1%)
    all_gather x1, waiting for transfers between devices, on_device(): cams = lax.all_gather(cam_tiles[0, 0], 'brick', axis=0, tiled=True)  55.1 us
    pallas_call x1, Pallas kernels, local_step(): pl.pallas_call(step_kernel, out_shape=(jax.ShapeDtypeStruct((bricks, size...  50.8 us
    ppermute x13, waiting for transfers between devices, swapped(): return lax.ppermute(value, axis, pairs)  40.2 us
    ppermute x13, starting transfers between devices, swapped(): return lax.ppermute(value, axis, pairs)  28.1 us
    all_to_all x1, starting transfers between devices, on_device(): lax.all_to_all(tile_sends[0, 0].reshape(shards, -1), 'brick', 0, 0, tiled...  12.7 us
    all_to_all x1, waiting for transfers between devices, on_device(): lax.all_to_all(tile_sends[0, 0].reshape(shards, -1), 'brick', 0, 0, tiled...  11.7 us
    unnamed x15, local copies, waits for them, and re-layouts  7.17 us
  transfers between devices with their start and end apart: 16, of which 15 were waited for; matrix products, arithmetic and copies ran while one was open for 2% of the time, Pallas kernels for 0%

profile of v2, /device:TPU:2, one launch (start us, length us, event | category | flops | bytes accessed | tf_op | source)
XLA Modules:
  0.0 229.5 jit_solution(16558879929823774470)
XLA Ops:
  7.9 1.9 collective-permute-start
  12.4 12.7 %all-to-all-start = ((s32[64,1,2]{2,1,0:T(1,128)}), s32[64,1,2]{2,1,0:T(1,128)S(1)}, u32[]{:S(2)}, u32[]{:S(2)}) async-start(s32[64,1,2]{2,1,0:T(1,128)} %bitcast), calls=%async_computation | async-start | bytes 65536 | tf_op jit(solution)/shard_map/all_to_all | solution.py:253
  27.8 11.7 %all-to-all-done = s32[64,1,2]{2,1,0:T(1,128)S(1)} async-done(((s32[64,1,2]{2,1,0:T(1,128)}), s32[64,1,2]{2,1,0:T(1,128)S(1)}, u32[]{:S(2)}, u32[]{:S(2)}) %all-to-all-start) | async-done | bytes 544 | tf_op jit(solution)/shard_map/all_to_all | solution.py:253
  40.4 55.1 %all-gather.3.cloned.1.call-done = bf16[1,1,256,64,256]{4,3,1,0,2:T(8,128)(2,1)} async-done(((bf16[1,1,4,64,256]{4,3,1,0,2:T(8,128)(2,1)}), bf16[1,1,256,64,256]{4,3,1,0,2:T(8,128)(2,1)}) %all-gather.3.cloned.1.call-update) | async-done | bytes 8388624 | tf_op jit(solution)/shard_map/all_gather | solution.py:252
  101.3 50.8 %voxel_step.1 = (bf16[24,128,256]{2,1,0:T(8,128)(2,1)}, f32[1024,256]{1,0:T(8,128)S(1)}) custom-call(s32[128]{0:T(128)S(1)} %reshape.13.sends, s32[192]{0:T(256)S(1)} %reshape_squeeze.4.entries, s32[1]{0:T(128)} %bitcast.10.shift, bf16[256,64,256]{2,1,0:T(8,128)(2,1)} %bitcast.14, bf16[24,128,256]{2,1,0:T(8,128)(2,1)S(1)} %collective-permute-done.behind, ...), custom_call_target="tpu_custom_call" | custom-call | tf_op jit(solution)/shard_map/voxel_step/pallas_call | solution.py:174
  155.7 2.4 %collective-permute-start.2 = (f32[256,256]{1,0:T(8,128)S(1)}, f32[256,256]{1,0:T(8,128)S(1)}, u32[]{:S(2)}, u32[]{:S(2)}) collective-permute-start(f32[256,256]{1,0:T(8,128)S(1)} %constant_dynamic-slice_fusion.3), channel_id=1, source_target_pairs={{0,16},{1,17},{2,18},{3,19},{4,20},{5,21},{6,22},{7,23},{8,24},{9,... | collective-permute-start | bytes 786440 | tf_op jit(solution)/shard_map/ppermute | solution.py:207
  158.1 6.6 %collective-permute-done.2 = f32[256,256]{1,0:T(8,128)S(1)} collective-permute-done((f32[256,256]{1,0:T(8,128)S(1)}, f32[256,256]{1,0:T(8,128)S(1)}, u32[]{:S(2)}, u32[]{:S(2)}) %collective-permute-start.2) | collective-permute-done | bytes 262176 | tf_op jit(solution)/shard_map/ppermute | solution.py:207
  165.7 4.1 %collective-permute-done.3 = f32[128,256]{1,0:T(8,128)S(1)} collective-permute-done((f32[128,256]{1,0:T(8,128)S(1)}, f32[128,256]{1,0:T(8,128)S(1)}, u32[]{:S(2)}, u32[]{:S(2)}) %collective-permute-start.3) | collective-permute-done | bytes 131104 | tf_op jit(solution)/shard_map/ppermute | solution.py:207
  169.8 2.2 collective-permute-start.4
  172.1 2.2 collective-permute-done.4
  174.3 2.4 %collective-permute-start.5 = (f32[32,256]{1,0:T(8,128)S(1)}, f32[32,256]{1,0:T(8,128)S(1)}, u32[]{:S(2)}, u32[]{:S(2)}) collective-permute-start(f32[32,256]{1,0:T(8,128)S(1)} %constant_dynamic-slice_fusion), channel_id=1, source_target_pairs={{0,4},{1,5},{2,6},{3,7},{4,0},{5,1},{6,2},{7,3},{8,12},{9,13},{10,... | collective-permute-start | bytes 98312 | tf_op jit(solution)/shard_map/ppermute | solution.py:207
  176.7 2.5 %collective-permute-done.5 = f32[32,256]{1,0:T(8,128)S(1)} collective-permute-done((f32[32,256]{1,0:T(8,128)S(1)}, f32[32,256]{1,0:T(8,128)S(1)}, u32[]{:S(2)}, u32[]{:S(2)}) %collective-permute-start.5) | collective-permute-done | bytes 32800 | tf_op jit(solution)/shard_map/ppermute | solution.py:207
  179.2 3.0 %collective-permute-start.6 = (f32[32,256]{1,0:T(8,128)S(1)}, f32[32,256]{1,0:T(8,128)S(1)}, u32[]{:S(2)}, u32[]{:S(2)}) collective-permute-start(f32[32,256]{1,0:T(8,128)S(1)} %dynamic-slice_add_fusion.4), channel_id=1, source_target_pairs={{0,12},{1,13},{2,14},{3,15},{4,8},{5,9},{6,10},{7,11},{8,4},{9,5},... | collective-permute-start | bytes 98312 | tf_op jit(solution)/shard_map/ppermute | solution.py:207
  182.3 3.0 %collective-permute-done.6 = f32[32,256]{1,0:T(8,128)S(1)} collective-permute-done((f32[32,256]{1,0:T(8,128)S(1)}, f32[32,256]{1,0:T(8,128)S(1)}, u32[]{:S(2)}, u32[]{:S(2)}) %collective-permute-start.6) | collective-permute-done | bytes 32800 | tf_op jit(solution)/shard_map/ppermute | solution.py:207
  185.3 3.5 %collective-permute-start.7 = (f32[32,256]{1,0:T(8,128)S(1)}, f32[32,256]{1,0:T(8,128)S(1)}, u32[]{:S(2)}, u32[]{:S(2)}) collective-permute-start(f32[32,256]{1,0:T(8,128)S(1)} %add.143), channel_id=1, source_target_pairs={{0,64},{64,0},{128,192},{192,128},{1,65},{65,1},{129,193},{193,129... | collective-permute-start | bytes 98312 | tf_op jit(solution)/shard_map/ppermute | solution.py:207
  190.7 2.7 %collective-permute-start.8 = (f32[32,256]{1,0:T(8,128)S(1)}, f32[32,256]{1,0:T(8,128)S(1)}, u32[]{:S(2)}, u32[]{:S(2)}) collective-permute-start(f32[32,256]{1,0:T(8,128)S(1)} %add.144), channel_id=1, source_target_pairs={{0,192},{64,128},{128,64},{192,0},{1,193},{65,129},{129,65},{193,1... | collective-permute-start | bytes 98312 | tf_op jit(solution)/shard_map/ppermute | solution.py:207
  193.3 2.5 %collective-permute-done.8 = f32[32,256]{1,0:T(8,128)S(1)} collective-permute-done((f32[32,256]{1,0:T(8,128)S(1)}, f32[32,256]{1,0:T(8,128)S(1)}, u32[]{:S(2)}, u32[]{:S(2)}) %collective-permute-start.8) | collective-permute-done | bytes 32800 | tf_op jit(solution)/shard_map/ppermute | solution.py:207
  195.8 2.3 %collective-permute-start.9 = (f32[32,256]{1,0:T(8,128)S(1)}, f32[32,256]{1,0:T(8,128)S(1)}, u32[]{:S(2)}, u32[]{:S(2)}) collective-permute-start(f32[32,256]{1,0:T(8,128)S(1)} %add.145), channel_id=1, source_target_pairs={{0,4},{1,5},{2,6},{3,7},{4,0},{5,1},{6,2},{7,3},{8,12},{9,13},{10,... | collective-permute-start | bytes 98312 | tf_op jit(solution)/shard_map/ppermute | solution.py:207
  198.1 2.5 %collective-permute-done.9 = f32[32,256]{1,0:T(8,128)S(1)} collective-permute-done((f32[32,256]{1,0:T(8,128)S(1)}, f32[32,256]{1,0:T(8,128)S(1)}, u32[]{:S(2)}, u32[]{:S(2)}) %collective-permute-start.9) | collective-permute-done | bytes 32800 | tf_op jit(solution)/shard_map/ppermute | solution.py:207
  202.2 2.8 %collective-permute-done.10 = f32[64,256]{1,0:T(8,128)S(1)} collective-permute-done((f32[64,256]{1,0:T(8,128)S(1)}, f32[64,256]{1,0:T(8,128)S(1)}, u32[]{:S(2)}, u32[]{:S(2)}) %collective-permute-start.10) | collective-permute-done | bytes 65568 | tf_op jit(solution)/shard_map/ppermute | solution.py:207
  205.8 4.3 %collective-permute-done.11 = f32[128,256]{1,0:T(8,128)S(1)} collective-permute-done((f32[128,256]{1,0:T(8,128)S(1)}, f32[128,256]{1,0:T(8,128)S(1)}, u32[]{:S(2)}, u32[]{:S(2)}) %collective-permute-start.11) | collective-permute-done | bytes 131104 | tf_op jit(solution)/shard_map/ppermute | solution.py:207
  210.1 4.4 %collective-permute-start.12 = (f32[256,256]{1,0:T(8,128)S(1)}, f32[256,256]{1,0:T(8,128)S(1)}, u32[]{:S(2)}, u32[]{:S(2)}) collective-permute-start(f32[256,256]{1,0:T(8,128)S(1)} %maximum_select_fusion.2), channel_id=1, source_target_pairs={{0,16},{1,17},{2,18},{3,19},{4,20},{5,21},{6,22},{7,23},{8,24},{9,... | collective-permute-start | bytes 786440 | tf_op jit(solution)/shard_map/ppermute | solution.py:207
  214.4 4.4 %collective-permute-done.12 = f32[256,256]{1,0:T(8,128)S(1)} collective-permute-done((f32[256,256]{1,0:T(8,128)S(1)}, f32[256,256]{1,0:T(8,128)S(1)}, u32[]{:S(2)}, u32[]{:S(2)}) %collective-permute-start.12) | collective-permute-done | bytes 262176 | tf_op jit(solution)/shard_map/ppermute | solution.py:207
  219.0 1.9 collective-permute-done.13
  (52 shorter events, 22.7 us)
Async XLA Ops:
  7.2 88.3 %all-gather.3.cloned.1.call-start = ((), (), s32[]{:S(2)}) async-start(), calls=%async_computation.1 | async-start | bytes 8519680 | tf_op jit(solution)/shard_map/all_gather | solution.py:252
  7.9 32.5 %collective-permute-start = (bf16[24,128,256]{2,1,0:T(8,128)(2,1)}, bf16[24,128,256]{2,1,0:T(8,128)(2,1)S(1)}, u32[]{:S(2)}, u32[]{:S(2)}) collective-permute-start(bf16[24,128,256]{2,1,0:T(8,128)(2,1)} %bitcast.11), channel_id=1, source_target_pairs={{0,1},{1,2},{2,3},{3,4},{4,5},{5,6},{6,7},{7,8},{8,9},{9,10},{10,1... | collective-permute-start | bytes 4718600 | tf_op jit(solution)/shard_map/ppermute | solution.py:256
  12.4 27.1 %all-to-all-start = ((s32[64,1,2]{2,1,0:T(1,128)}), s32[64,1,2]{2,1,0:T(1,128)S(1)}, u32[]{:S(2)}, u32[]{:S(2)}) async-start(s32[64,1,2]{2,1,0:T(1,128)} %bitcast), calls=%async_computation | async-start | bytes 65536 | tf_op jit(solution)/shard_map/all_to_all | solution.py:253
  95.5 1.4 copy-start
  96.9 0.9 copy-start.1
  97.8 0.9 copy-start.2
  98.8 0.9 copy-start.3
  99.7 0.9 copy-start.4
  100.6 0.7 copy-start.5
  152.1 3.4 %collective-permute-start.1 = (f32[512,256]{1,0:T(8,128)S(1)}, f32[512,256]{1,0:T(8,128)S(1)}, u32[]{:S(2)}, u32[]{:S(2)}) collective-permute-start(f32[512,256]{1,0:T(8,128)S(1)} %constant_dynamic-slice_fusion.4), channel_id=1, source_target_pairs={{0,1},{1,0},{2,3},{3,2},{4,5},{5,4},{6,7},{7,6},{8,9},{9,8},{10,11... | collective-permute-start | bytes 1572872 | tf_op jit(solution)/shard_map/ppermute | solution.py:207
  155.7 9.0 %collective-permute-start.2 = (f32[256,256]{1,0:T(8,128)S(1)}, f32[256,256]{1,0:T(8,128)S(1)}, u32[]{:S(2)}, u32[]{:S(2)}) collective-permute-start(f32[256,256]{1,0:T(8,128)S(1)} %constant_dynamic-slice_fusion.3), channel_id=1, source_target_pairs={{0,16},{1,17},{2,18},{3,19},{4,20},{5,21},{6,22},{7,23},{8,24},{9,... | collective-permute-start | bytes 786440 | tf_op jit(solution)/shard_map/ppermute | solution.py:207
  164.7 5.1 %collective-permute-start.3 = (f32[128,256]{1,0:T(8,128)S(1)}, f32[128,256]{1,0:T(8,128)S(1)}, u32[]{:S(2)}, u32[]{:S(2)}) collective-permute-start(f32[128,256]{1,0:T(8,128)S(1)} %constant_dynamic-slice_fusion.2), channel_id=1, source_target_pairs={{0,48},{1,49},{2,50},{3,51},{4,52},{5,53},{6,54},{7,55},{8,56},{9,... | collective-permute-start | bytes 393224 | tf_op jit(solution)/shard_map/ppermute | solution.py:207
  169.8 4.5 %collective-permute-start.4 = (f32[64,256]{1,0:T(8,128)S(1)}, f32[64,256]{1,0:T(8,128)S(1)}, u32[]{:S(2)}, u32[]{:S(2)}) collective-permute-start(f32[64,256]{1,0:T(8,128)S(1)} %constant_dynamic-slice_fusion.1), channel_id=1, source_target_pairs={{0,2},{1,3},{2,0},{3,1},{4,6},{5,7},{6,4},{7,5},{8,10},{9,11},{10,... | collective-permute-start | bytes 196616 | tf_op jit(solution)/shard_map/ppermute | solution.py:207
  174.3 4.9 %collective-permute-start.5 = (f32[32,256]{1,0:T(8,128)S(1)}, f32[32,256]{1,0:T(8,128)S(1)}, u32[]{:S(2)}, u32[]{:S(2)}) collective-permute-start(f32[32,256]{1,0:T(8,128)S(1)} %constant_dynamic-slice_fusion), channel_id=1, source_target_pairs={{0,4},{1,5},{2,6},{3,7},{4,0},{5,1},{6,2},{7,3},{8,12},{9,13},{10,... | collective-permute-start | bytes 98312 | tf_op jit(solution)/shard_map/ppermute | solution.py:207
  179.2 6.0 %collective-permute-start.6 = (f32[32,256]{1,0:T(8,128)S(1)}, f32[32,256]{1,0:T(8,128)S(1)}, u32[]{:S(2)}, u32[]{:S(2)}) collective-permute-start(f32[32,256]{1,0:T(8,128)S(1)} %dynamic-slice_add_fusion.4), channel_id=1, source_target_pairs={{0,12},{1,13},{2,14},{3,15},{4,8},{5,9},{6,10},{7,11},{8,4},{9,5},... | collective-permute-start | bytes 98312 | tf_op jit(solution)/shard_map/ppermute | solution.py:207
  185.3 5.4 %collective-permute-start.7 = (f32[32,256]{1,0:T(8,128)S(1)}, f32[32,256]{1,0:T(8,128)S(1)}, u32[]{:S(2)}, u32[]{:S(2)}) collective-permute-start(f32[32,256]{1,0:T(8,128)S(1)} %add.143), channel_id=1, source_target_pairs={{0,64},{64,0},{128,192},{192,128},{1,65},{65,1},{129,193},{193,129... | collective-permute-start | bytes 98312 | tf_op jit(solution)/shard_map/ppermute | solution.py:207
  190.7 5.1 %collective-permute-start.8 = (f32[32,256]{1,0:T(8,128)S(1)}, f32[32,256]{1,0:T(8,128)S(1)}, u32[]{:S(2)}, u32[]{:S(2)}) collective-permute-start(f32[32,256]{1,0:T(8,128)S(1)} %add.144), channel_id=1, source_target_pairs={{0,192},{64,128},{128,64},{192,0},{1,193},{65,129},{129,65},{193,1... | collective-permute-start | bytes 98312 | tf_op jit(solution)/shard_map/ppermute | solution.py:207
  195.8 4.8 %collective-permute-start.9 = (f32[32,256]{1,0:T(8,128)S(1)}, f32[32,256]{1,0:T(8,128)S(1)}, u32[]{:S(2)}, u32[]{:S(2)}) collective-permute-start(f32[32,256]{1,0:T(8,128)S(1)} %add.145), channel_id=1, source_target_pairs={{0,4},{1,5},{2,6},{3,7},{4,0},{5,1},{6,2},{7,3},{8,12},{9,13},{10,... | collective-permute-start | bytes 98312 | tf_op jit(solution)/shard_map/ppermute | solution.py:207
  200.6 4.4 %collective-permute-start.10 = (f32[64,256]{1,0:T(8,128)S(1)}, f32[64,256]{1,0:T(8,128)S(1)}, u32[]{:S(2)}, u32[]{:S(2)}) collective-permute-start(f32[64,256]{1,0:T(8,128)S(1)} %maximum_select_fusion.4), channel_id=1, source_target_pairs={{0,2},{1,3},{2,0},{3,1},{4,6},{5,7},{6,4},{7,5},{8,10},{9,11},{10,... | collective-permute-start | bytes 196616 | tf_op jit(solution)/shard_map/ppermute | solution.py:207
  205.0 5.1 %collective-permute-start.11 = (f32[128,256]{1,0:T(8,128)S(1)}, f32[128,256]{1,0:T(8,128)S(1)}, u32[]{:S(2)}, u32[]{:S(2)}) collective-permute-start(f32[128,256]{1,0:T(8,128)S(1)} %maximum_select_fusion.3), channel_id=1, source_target_pairs={{0,48},{1,49},{2,50},{3,51},{4,52},{5,53},{6,54},{7,55},{8,56},{9,... | collective-permute-start | bytes 393224 | tf_op jit(solution)/shard_map/ppermute | solution.py:207
  210.1 8.7 %collective-permute-start.12 = (f32[256,256]{1,0:T(8,128)S(1)}, f32[256,256]{1,0:T(8,128)S(1)}, u32[]{:S(2)}, u32[]{:S(2)}) collective-permute-start(f32[256,256]{1,0:T(8,128)S(1)} %maximum_select_fusion.2), channel_id=1, source_target_pairs={{0,16},{1,17},{2,18},{3,19},{4,20},{5,21},{6,22},{7,23},{8,24},{9,... | collective-permute-start | bytes 786440 | tf_op jit(solution)/shard_map/ppermute | solution.py:207
  218.8 2.0 collective-permute-start.13
Sparse Core Ops, SparseCore 0:
  10.7 84.6 all-gather.2

commit v3 on v2

--- a/solution.py
+++ b/solution.py
@@ -22,11 +22,22 @@
     return values * lax.rsqrt(mean_sq + 1e-06) * norm_gain
 
 
-def step_kernel(
-    sends,
+def step_kernel(sources, me, entries, shift, *refs):
+    brick_kernel(sources, me, entries, shift, refs[: len(sources)], *refs[len(sources) :])
+
+
+def shard_of(me, source):
+    x, z, core = me // 16, me // 2 % 8, me % 2
+    mask_x, mask_z, step_z, swap = source
+    return (x ^ mask_x) * 16 + (((z ^ mask_z) + step_z) % 8) * 2 + (core ^ swap)
+
+
+def brick_kernel(
+    sources,
+    me,
     entries,
     shift,
-    cams,
+    pieces,
     behind,
     prev,
     vox,
@@ -44,19 +55,30 @@
     query_s,
     att_s,
     feat_s,
+    cams,
+    plan_v,
+    plan,
+    sem,
 ):
     step = pl.program_id(0)
     bricks = prev.shape[0]
     size = prev.shape[1]
     width = prev.shape[2]
     list_len = entries.shape[0] // bricks
-    pixels = cams.shape[1]
-    tile_dev = cams.shape[0] // (sends.shape[0] // 2)
+    pixels = feat_s.shape[0] // list_len
+    own = me[0]
     rows = GROUP * size
     log2_scale = 1.4426950408889634 / HD**0.5
 
     @pl.when(step == 0)
     def _():
+        for piece, (first_row, blocks) in zip(pieces, sources):
+            for at, source in enumerate(blocks):
+                pltpu.make_async_copy(
+                    piece.at[at],
+                    cams.at[shard_of(own, source), pl.ds(first_row, piece.shape[1]), :],
+                    sem,
+                ).start()
         grads[...] = jnp.zeros_like(grads)
         feat_s[...] = jnp.zeros_like(feat_s)
 
@@ -72,6 +94,13 @@
         normed = rms_norm(q_in, gains[0:1, :]).astype(jnp.bfloat16)
         query_s[here, :] = dot(normed, w_query[...]).astype(jnp.bfloat16)
 
+    @pl.when(step == 0)
+    def _():
+        pltpu.make_async_copy(cams, cams, sem).wait()
+        table = cams[:, pl.ds(FIRST * pixels, 16), pl.ds(0, 128)].astype(jnp.float32)
+        plan_v[...] = jnp.sum(table, axis=1).astype(jnp.int32)
+        pltpu.sync_copy(plan_v, plan)
+
     lane_head = lax.broadcasted_iota(jnp.int32, (size, width), 1) // HD
 
     def one_brick(g, carry):
@@ -82,8 +111,11 @@
 
             @pl.when(entry >= 0)
             def _(entry=entry, live=live):
-                tile = (entry // 2) * tile_dev + sends[entry]
-                feat_s[pl.ds(pl.multiple_of(live * pixels, pixels), pixels), :] = cams[tile]
+                local = plan[entry // 2, own * 2 + entry % 2]
+                row = local * pixels + jnp.where(local >= FIRST, 16, 0)
+                feat_s[pl.ds(pl.multiple_of(live * pixels, pixels), pixels), :] = cams[
+                    entry // 2, pl.ds(pl.multiple_of(row, 16), pixels), :
+                ]
 
             live = live + (entry >= 0).astype(jnp.int32)
         here = pl.ds(pl.multiple_of(g * size, size), size)
@@ -143,7 +175,7 @@
 
 
 def local_step(
-    sends, entries, shift, cams, behind, prev, vox, cot, gains, w_query, w_keyval, w_attn_out,
+    me, entries, shift, pieces, sources, pixels, behind, prev, vox, cot, gains, w_query, w_keyval, w_attn_out,
     w_in, w_out, interpret=False,
 ):
     bricks, size, width = prev.shape
@@ -157,7 +189,6 @@
 
     block = pl.BlockSpec((GROUP, size, width), lambda i, *_: (i, 0, 0))
     operands = (
-        cams,
         behind,
         prev,
         vox,
@@ -170,9 +201,12 @@
         w_in,
         w_out,
     )
-    specs = [block if a is vox or a is cot else whole(a) for a in operands]
+    specs = [pl.BlockSpec(memory_space=pltpu.HBM)] * len(pieces)
+    specs += [block if a is vox or a is cot else whole(a) for a in operands]
+    shards = sum(len(blocks) for first_row, blocks in sources if first_row == 0)
+    per_shard = sum({f: p.shape[1] for p, (f, _) in zip(pieces, sources)}.values())
     return pl.pallas_call(
-        step_kernel,
+        functools.partial(step_kernel, sources),
         out_shape=(
             jax.ShapeDtypeStruct((bricks, size, width), jnp.bfloat16),
             jax.ShapeDtypeStruct((2 * hidden, width), jnp.float32),
@@ -189,13 +223,17 @@
                 pltpu.VMEM((rows, width), jnp.float32),
                 pltpu.VMEM((rows, width), jnp.bfloat16),
                 pltpu.VMEM((rows, width), jnp.bfloat16),
-                pltpu.VMEM((list_len * cams.shape[1], width), jnp.bfloat16),
+                pltpu.VMEM((list_len * pixels, width), jnp.bfloat16),
+                pltpu.VMEM((shards, per_shard, width), jnp.bfloat16),
+                pltpu.VMEM((shards, 128), jnp.int32),
+                pltpu.SMEM((shards, 128), jnp.int32),
+                pltpu.SemaphoreType.DMA,
             ],
         ),
-        compiler_params=pltpu.CompilerParams(vmem_limit_bytes=48 << 20),
+        compiler_params=pltpu.CompilerParams(vmem_limit_bytes=60 * 1024 * 1024),
         name="voxel_step",
         interpret=interpret,
-    )(sends, entries, shift, *operands)
+    )(me, entries, shift, *pieces, *operands)
 
 
 SCATTER = ((1, 1), (16, 48), (48, 32), (2, 2), (4, 12))
@@ -232,6 +270,54 @@
     return value
 
 
+FIRST = 4
+
+
+def along_z(value, step):
+    def target(i):
+        return i // 16 * 16 + (i // 2 + step) % 8 * 2 + i % 2
+
+    return lax.ppermute(value, "brick", [(i, target(i)) for i in range(64)])
+
+
+def gathered(tiles, sends):
+    width = tiles.shape[-1]
+    table = jnp.pad(sends.astype(tiles.dtype), ((0, 15), (0, width - sends.shape[1])))
+    first = jnp.concatenate([tiles[:FIRST].reshape(-1, width), table], 0)[None]
+    found = []
+
+    first = jnp.concatenate([first, swapped(first, "brick", 16)], 0)
+    first = jnp.concatenate([first, swapped(first, "brick", 48)], 0)
+    xs = (0, 1, 3, 2)
+    found.append((first, 0, [(m, 0, 0, 0) for m in xs]))
+    for way, count in ((1, 3), (-1, 4)):
+        block = first
+        for k in range(1, count + 1):
+            block = along_z(block, way)
+            found.append((block, 0, [(m, 0, -way * k, 0) for m in xs]))
+
+    if FIRST < tiles.shape[0]:
+        row = first.shape[1]
+        second = tiles[FIRST:].reshape(1, -1, width)
+        for mask in (2, 4, 12):
+            second = jnp.concatenate([second, swapped(second, "brick", mask)], 0)
+        zs = (0, 1, 2, 3, 6, 7, 4, 5)
+        third = swapped(second, "brick", 16)
+        for block, m in (
+            (second, 0),
+            (third, 1),
+            (swapped(second, "brick", 48), 3),
+            (swapped(third, "brick", 48), 2),
+        ):
+            found.append((block, row, [(m, n, 0, 0) for n in zs]))
+
+    found += [
+        (swapped(block, "brick", 1), row, [(a, b, c, 1) for a, b, c, _ in blocks])
+        for block, row, blocks in found
+    ]
+    return [f[0] for f in found], [f[1:] for f in found]
+
+
 def on_device(
     cam_tiles,
     vox_embed,
@@ -249,16 +335,16 @@
 ):
     shards = lax.axis_size("brick")
     prev = prev_state[0]
-    cams = lax.all_gather(cam_tiles[0, 0], "brick", axis=0, tiled=True)
-    own_plan = lax.all_to_all(
-        tile_sends[0, 0].reshape(shards, -1), "brick", 0, 0, tiled=True
-    ).reshape(-1)
     behind = lax.ppermute(prev, "brick", [(i, i + 1) for i in range(shards - 1)])
+    pixels = cam_tiles.shape[3]
+    pieces, sources = gathered(cam_tiles[0, 0], tile_sends[0, 0])
     new_state, grads = local_step(
-        own_plan,
+        lax.axis_index("brick").reshape(1),
         brick_tiles[0, 0].reshape(-1),
         ego_shift[0],
-        cams,
+        pieces,
+        sources,
+        pixels,
         behind,
         prev,
         vox_embed,

time: 232 us -> 223 us (0.961)
  waiting for transfers between devices: 108 us -> 83.9 us
  starting transfers between devices: 42.8 us -> 65.7 us
  between operations: 14.9 us -> 1.67 us
  Pallas kernels: 50.8 us -> 58.1 us
  local copies, waits for them, and re-layouts: 10.1 us -> 6.35 us
    all_gather x1 -> x0, waiting for transfers between devices: 55.1 us -> none  [on_device(): cams = lax.all_gather(cam_tiles[0, 0], 'brick', axis=0, tiled=True)]
    ppermute x0 -> x7, waiting for transfers between devices: none -> 25.6 us  [along_z(): return lax.ppermute(value, 'brick', [(i, target(i)) for i in range(64)])]
    ppermute x13 -> x23, starting transfers between devices: 28.1 us -> 46.4 us  [swapped(): return lax.ppermute(value, axis, pairs)]
    ppermute x13 -> x23, waiting for transfers between devices: 40.2 us -> 58.3 us  [swapped(): return lax.ppermute(value, axis, pairs)]
    ppermute x0 -> x7, starting transfers between devices: none -> 17.4 us  [along_z(): return lax.ppermute(value, 'brick', [(i, target(i)) for i in range(64)])]
    all_to_all x1 -> x0, starting transfers between devices: 12.7 us -> none  [on_device(): lax.all_to_all(tile_sends[0, 0].reshape(shards, -1), 'brick', 0, 0, tiled...]
    all_to_all x1 -> x0, waiting for transfers between devices: 11.7 us -> none  [on_device(): lax.all_to_all(tile_sends[0, 0].reshape(shards, -1), 'brick', 0, 0, tiled...]
    pallas_call x1, Pallas kernels: 50.8 us -> 58.1 us  [local_step(): pl.pallas_call(functools.partial(step_kernel, sources), out_shape=(jax.Sh...]
  transfers between devices with their start and end apart: 16 -> 31, of which waited for: 15 -> 19; matrix products, arithmetic and copies ran while one was open for 2% -> 1% of each run, Pallas kernels for 0% -> 0%
where the time goes in v3:
time: 223 us; the launch traced here: 220 us
  waiting for transfers between devices  83.9 us (38%)
  starting transfers between devices  65.7 us (29%)
  Pallas kernels  58.1 us (26%)
  local copies, waits for them, and re-layouts  6.35 us (3%)
  other arithmetic  3.98 us (2%)
    ppermute x23, waiting for transfers between devices, swapped(): return lax.ppermute(value, axis, pairs)  58.3 us
    pallas_call x1, Pallas kernels, local_step(): pl.pallas_call(functools.partial(step_kernel, sources), out_shape=(jax.Sh...  58.1 us
    ppermute x23, starting transfers between devices, swapped(): return lax.ppermute(value, axis, pairs)  46.4 us
    ppermute x7, waiting for transfers between devices, along_z(): return lax.ppermute(value, 'brick', [(i, target(i)) for i in range(64)])  25.6 us
    ppermute x7, starting transfers between devices, along_z(): return lax.ppermute(value, 'brick', [(i, target(i)) for i in range(64)])  17.4 us
  transfers between devices with their start and end apart: 31, of which 19 were waited for; matrix products, arithmetic and copies ran while one was open for 1% of the time, Pallas kernels for 0%

profile of v3, /device:TPU:2, one launch (start us, length us, event | category | flops | bytes accessed | tf_op | source)
XLA Modules:
  0.0 219.7 jit_solution(17888366241185296651)
XLA Ops:
  4.7 3.2 %collective-permute-done = bf16[1,272,256]{2,1,0:T(8,128)(2,1)S(1)} collective-permute-done((bf16[1,272,256]{2,1,0:T(8,128)(2,1)S(1)}, bf16[1,272,256]{2,1,0:T(8,128)(2,1)S(1)}, u32[]{:S(2)}, u32[]{:S(2)}) %collective-permute-start) | collective-permute-done | bytes 139296 | tf_op jit(solution)/shard_map/ppermute | solution.py:245
  9.5 5.8 %collective-permute-done.1 = bf16[2,272,256]{2,1,0:T(8,128)(2,1)S(1)} collective-permute-done((bf16[2,272,256]{2,1,0:T(8,128)(2,1)S(1)}, bf16[2,272,256]{2,1,0:T(8,128)(2,1)S(1)}, u32[]{:S(2)}, u32[]{:S(2)}) %collective-permute-start.1) | collective-permute-done | bytes 278560 | tf_op jit(solution)/shard_map/ppermute | solution.py:245
  15.4 6.2 %collective-permute-start.5 = (bf16[4,272,256]{2,1,0:T(8,128)(2,1)S(1)}, bf16[4,272,256]{2,1,0:T(8,128)(2,1)S(1)}, u32[]{:S(2)}, u32[]{:S(2)}) collective-permute-start(bf16[4,272,256]{2,1,0:T(8,128)(2,1)S(1)} %pad_maximum_fusion.refs_0_), channel_id=1, source_target_pairs={{0,14},{1,15},{2,0},{3,1},{4,2},{5,3},{6,4},{7,5},{8,6},{9,7},{10,... | collective-permute-start | bytes 1671176 | tf_op jit(solution)/shard_map/ppermute | solution.py:280
  21.5 10.2 %collective-permute-done.5.refs_4_ = bf16[4,272,256]{2,1,0:T(8,128)(2,1)S(1)} collective-permute-done((bf16[4,272,256]{2,1,0:T(8,128)(2,1)S(1)}, bf16[4,272,256]{2,1,0:T(8,128)(2,1)S(1)}, u32[]{:S(2)}, u32[]{:S(2)}) %collective-permute-start.5) | collective-permute-done | bytes 557088 | tf_op jit(solution)/shard_map/ppermute | solution.py:280
  31.7 3.7 %collective-permute-start.6 = (bf16[4,272,256]{2,1,0:T(8,128)(2,1)S(1)}, bf16[4,272,256]{2,1,0:T(8,128)(2,1)}, u32[]{:S(2)}, u32[]{:S(2)}) collective-permute-start(bf16[4,272,256]{2,1,0:T(8,128)(2,1)S(1)} %collective-permute-done.5.refs_4_), channel_id=1, source_target_pairs={{0,14},{1,15},{2,0},{3,1},{4,2},{5,3},{6,4},{7,5},{8,6},{9,7},{10,... | collective-permute-start | bytes 1671176 | tf_op jit(solution)/shard_map/ppermute | solution.py:280
  37.5 7.2 %collective-permute-done.6.refs_5_ = bf16[4,272,256]{2,1,0:T(8,128)(2,1)} collective-permute-done((bf16[4,272,256]{2,1,0:T(8,128)(2,1)S(1)}, bf16[4,272,256]{2,1,0:T(8,128)(2,1)}, u32[]{:S(2)}, u32[]{:S(2)}) %collective-permute-start.6) | collective-permute-done | bytes 557088 | tf_op jit(solution)/shard_map/ppermute | solution.py:280
  44.7 3.8 %collective-permute-start.7 = (bf16[4,272,256]{2,1,0:T(8,128)(2,1)}, bf16[4,272,256]{2,1,0:T(8,128)(2,1)}, u32[]{:S(2)}, u32[]{:S(2)}) collective-permute-start(bf16[4,272,256]{2,1,0:T(8,128)(2,1)} %collective-permute-done.6.refs_5_), channel_id=1, source_target_pairs={{0,14},{1,15},{2,0},{3,1},{4,2},{5,3},{6,4},{7,5},{8,6},{9,7},{10,... | collective-permute-start | bytes 1671176 | tf_op jit(solution)/shard_map/ppermute | solution.py:280
  49.0 6.2 %collective-permute-done.3.refs_2_ = bf16[4,272,256]{2,1,0:T(8,128)(2,1)} collective-permute-done((bf16[4,272,256]{2,1,0:T(8,128)(2,1)S(1)}, bf16[4,272,256]{2,1,0:T(8,128)(2,1)}, u32[]{:S(2)}, u32[]{:S(2)}) %collective-permute-start.3) | collective-permute-done | bytes 557088 | tf_op jit(solution)/shard_map/ppermute | solution.py:280
  57.3 3.7 %collective-permute-start.8 = (bf16[4,272,256]{2,1,0:T(8,128)(2,1)}, bf16[4,272,256]{2,1,0:T(8,128)(2,1)}, u32[]{:S(2)}, u32[]{:S(2)}) collective-permute-start(bf16[4,272,256]{2,1,0:T(8,128)(2,1)} %collective-permute-done.7.refs_6_), channel_id=1, source_target_pairs={{0,14},{1,15},{2,0},{3,1},{4,2},{5,3},{6,4},{7,5},{8,6},{9,7},{10,... | collective-permute-start | bytes 1671176 | tf_op jit(solution)/shard_map/ppermute | solution.py:280
  61.0 18.8 %collective-permute-start.11 = (bf16[4,272,256]{2,1,0:T(8,128)(2,1)}, bf16[4,272,256]{2,1,0:T(8,128)(2,1)}, u32[]{:S(2)}, u32[]{:S(2)}) collective-permute-start(bf16[4,272,256]{2,1,0:T(8,128)(2,1)} %collective-permute-done.3.refs_2_), channel_id=1, source_target_pairs={{0,1},{1,0},{2,3},{3,2},{4,5},{5,4},{6,7},{7,6},{8,9},{9,8},{10,11... | collective-permute-start | bytes 1671176 | tf_op jit(solution)/shard_map/ppermute | solution.py:245
  81.5 5.5 %collective-permute-start.12 = (bf16[4,272,256]{2,1,0:T(8,128)(2,1)}, bf16[4,272,256]{2,1,0:T(8,128)(2,1)S(1)}, u32[]{:S(2)}, u32[]{:S(2)}) collective-permute-start(bf16[4,272,256]{2,1,0:T(8,128)(2,1)} %collective-permute-done.4.refs_3_), channel_id=1, source_target_pairs={{0,1},{1,0},{2,3},{3,2},{4,5},{5,4},{6,7},{7,6},{8,9},{9,8},{10,11... | collective-permute-start | bytes 1671176 | tf_op jit(solution)/shard_map/ppermute | solution.py:245
  91.1 58.1 %voxel_step.1 = (bf16[24,128,256]{2,1,0:T(8,128)(2,1)}, f32[1024,256]{1,0:T(8,128)}) custom-call(s32[1]{0:T(128)} %bitcast.me, s32[192]{0:T(256)} %reshape_squeeze.6.entries, s32[1]{0:T(128)} %bitcast.13.shift, bf16[4,272,256]{2,1,0:T(8,128)(2,1)} %copy-done, bf16[4,272,256]{2,1,0:T(8,128)(2,1)} %copy-done.4, ...), custom_call_target="tpu_custom_call" | custom-call | tf_op jit(solution)/shard_map/voxel_step/pallas_call | solution.py:208
  154.0 7.9 %collective-permute-done.19 = f32[256,256]{1,0:T(8,128)S(1)} collective-permute-done((f32[256,256]{1,0:T(8,128)S(1)}, f32[256,256]{1,0:T(8,128)S(1)}, u32[]{:S(2)}, u32[]{:S(2)}) %collective-permute-start.19) | collective-permute-done | bytes 262176 | tf_op jit(solution)/shard_map/ppermute | solution.py:245
  164.2 2.9 %collective-permute-done.20 = f32[128,256]{1,0:T(8,128)S(1)} collective-permute-done((f32[128,256]{1,0:T(8,128)S(1)}, f32[128,256]{1,0:T(8,128)S(1)}, u32[]{:S(2)}, u32[]{:S(2)}) %collective-permute-start.20) | collective-permute-done | bytes 131104 | tf_op jit(solution)/shard_map/ppermute | solution.py:245
  168.0 3.6 %collective-permute-done.21 = f32[64,256]{1,0:T(8,128)S(1)} collective-permute-done((f32[64,256]{1,0:T(8,128)S(1)}, f32[64,256]{1,0:T(8,128)S(1)}, u32[]{:S(2)}, u32[]{:S(2)}) %collective-permute-start.21) | collective-permute-done | bytes 65568 | tf_op jit(solution)/shard_map/ppermute | solution.py:245
  172.0 5.0 %collective-permute-done.22 = f32[32,256]{1,0:T(8,128)S(1)} collective-permute-done((f32[32,256]{1,0:T(8,128)S(1)}, f32[32,256]{1,0:T(8,128)S(1)}, u32[]{:S(2)}, u32[]{:S(2)}) %collective-permute-start.22) | collective-permute-done | bytes 32800 | tf_op jit(solution)/shard_map/ppermute | solution.py:245
  177.2 5.8 %collective-permute-done.23 = f32[32,256]{1,0:T(8,128)S(1)} collective-permute-done((f32[32,256]{1,0:T(8,128)S(1)}, f32[32,256]{1,0:T(8,128)S(1)}, u32[]{:S(2)}, u32[]{:S(2)}) %collective-permute-start.23) | collective-permute-done | bytes 32800 | tf_op jit(solution)/shard_map/ppermute | solution.py:245
  183.0 3.1 %collective-permute-start.24 = (f32[32,256]{1,0:T(8,128)S(1)}, f32[32,256]{1,0:T(8,128)S(1)}, u32[]{:S(2)}, u32[]{:S(2)}) collective-permute-start(f32[32,256]{1,0:T(8,128)S(1)} %add.145), channel_id=1, source_target_pairs={{0,64},{64,0},{128,192},{192,128},{1,65},{65,1},{129,193},{193,129... | collective-permute-start | bytes 98312 | tf_op jit(solution)/shard_map/ppermute | solution.py:245
  188.0 2.9 %collective-permute-start.25 = (f32[32,256]{1,0:T(8,128)S(1)}, f32[32,256]{1,0:T(8,128)S(1)}, u32[]{:S(2)}, u32[]{:S(2)}) collective-permute-start(f32[32,256]{1,0:T(8,128)S(1)} %add.146), channel_id=1, source_target_pairs={{0,192},{64,128},{128,64},{192,0},{1,193},{65,129},{129,65},{193,1... | collective-permute-start | bytes 98312 | tf_op jit(solution)/shard_map/ppermute | solution.py:245
  193.4 4.6 %collective-permute-done.26 = f32[32,256]{1,0:T(8,128)S(1)} collective-permute-done((f32[32,256]{1,0:T(8,128)S(1)}, f32[32,256]{1,0:T(8,128)S(1)}, u32[]{:S(2)}, u32[]{:S(2)}) %collective-permute-start.26) | collective-permute-done | bytes 32800 | tf_op jit(solution)/shard_map/ppermute | solution.py:245
  198.3 4.1 %collective-permute-done.27 = f32[64,256]{1,0:T(8,128)S(1)} collective-permute-done((f32[64,256]{1,0:T(8,128)S(1)}, f32[64,256]{1,0:T(8,128)S(1)}, u32[]{:S(2)}, u32[]{:S(2)}) %collective-permute-start.27) | collective-permute-done | bytes 65568 | tf_op jit(solution)/shard_map/ppermute | solution.py:245
  204.1 3.3 %collective-permute-done.28 = f32[128,256]{1,0:T(8,128)S(1)} collective-permute-done((f32[128,256]{1,0:T(8,128)S(1)}, f32[128,256]{1,0:T(8,128)S(1)}, u32[]{:S(2)}, u32[]{:S(2)}) %collective-permute-start.28) | collective-permute-done | bytes 131104 | tf_op jit(solution)/shard_map/ppermute | solution.py:245
  207.4 4.1 %collective-permute-start.29 = (f32[256,256]{1,0:T(8,128)S(1)}, f32[256,256]{1,0:T(8,128)S(1)}, u32[]{:S(2)}, u32[]{:S(2)}) collective-permute-start(f32[256,256]{1,0:T(8,128)S(1)} %maximum_select_fusion.2), channel_id=1, source_target_pairs={{0,16},{1,17},{2,18},{3,19},{4,20},{5,21},{6,22},{7,23},{8,24},{9,... | collective-permute-start | bytes 786440 | tf_op jit(solution)/shard_map/ppermute | solution.py:245
  211.5 4.4 %collective-permute-done.29 = f32[256,256]{1,0:T(8,128)S(1)} collective-permute-done((f32[256,256]{1,0:T(8,128)S(1)}, f32[256,256]{1,0:T(8,128)S(1)}, u32[]{:S(2)}, u32[]{:S(2)}) %collective-permute-start.29) | collective-permute-done | bytes 262176 | tf_op jit(solution)/shard_map/ppermute | solution.py:245
  (92 shorter events, 34.1 us)
Async XLA Ops:
  2.4 5.5 %collective-permute-start = (bf16[1,272,256]{2,1,0:T(8,128)(2,1)S(1)}, bf16[1,272,256]{2,1,0:T(8,128)(2,1)S(1)}, u32[]{:S(2)}, u32[]{:S(2)}) collective-permute-start(bf16[1,272,256]{2,1,0:T(8,128)(2,1)S(1)} %fusion.2), channel_id=1, source_target_pairs={{0,16},{1,17},{2,18},{3,19},{4,20},{5,21},{6,22},{7,23},{8,24},{9,... | collective-permute-start | bytes 417800 | tf_op jit(solution)/shard_map/ppermute | solution.py:245
  7.9 7.4 %collective-permute-start.1 = (bf16[2,272,256]{2,1,0:T(8,128)(2,1)S(1)}, bf16[2,272,256]{2,1,0:T(8,128)(2,1)S(1)}, u32[]{:S(2)}, u32[]{:S(2)}) collective-permute-start(bf16[2,272,256]{2,1,0:T(8,128)(2,1)S(1)} %pad_maximum_fusion.2), channel_id=1, source_target_pairs={{0,48},{1,49},{2,50},{3,51},{4,52},{5,53},{6,54},{7,55},{8,56},{9,... | collective-permute-start | bytes 835592 | tf_op jit(solution)/shard_map/ppermute | solution.py:245
  15.4 16.3 %collective-permute-start.5 = (bf16[4,272,256]{2,1,0:T(8,128)(2,1)S(1)}, bf16[4,272,256]{2,1,0:T(8,128)(2,1)S(1)}, u32[]{:S(2)}, u32[]{:S(2)}) collective-permute-start(bf16[4,272,256]{2,1,0:T(8,128)(2,1)S(1)} %pad_maximum_fusion.refs_0_), channel_id=1, source_target_pairs={{0,14},{1,15},{2,0},{3,1},{4,2},{5,3},{6,4},{7,5},{8,6},{9,7},{10,... | collective-permute-start | bytes 1671176 | tf_op jit(solution)/shard_map/ppermute | solution.py:280
  21.5 15.9 %collective-permute-start.2 = (bf16[4,272,256]{2,1,0:T(8,128)(2,1)S(1)}, bf16[4,272,256]{2,1,0:T(8,128)(2,1)S(1)}, u32[]{:S(2)}, u32[]{:S(2)}) collective-permute-start(bf16[4,272,256]{2,1,0:T(8,128)(2,1)S(1)} %pad_maximum_fusion.refs_0_), channel_id=1, source_target_pairs={{0,2},{1,3},{2,4},{3,5},{4,6},{5,7},{6,8},{7,9},{8,10},{9,11},{10,... | collective-permute-start | bytes 1671176 | tf_op jit(solution)/shard_map/ppermute | solution.py:280
  31.7 13.0 %collective-permute-start.6 = (bf16[4,272,256]{2,1,0:T(8,128)(2,1)S(1)}, bf16[4,272,256]{2,1,0:T(8,128)(2,1)}, u32[]{:S(2)}, u32[]{:S(2)}) collective-permute-start(bf16[4,272,256]{2,1,0:T(8,128)(2,1)S(1)} %collective-permute-done.5.refs_4_), channel_id=1, source_target_pairs={{0,14},{1,15},{2,0},{3,1},{4,2},{5,3},{6,4},{7,5},{8,6},{9,7},{10,... | collective-permute-start | bytes 1671176 | tf_op jit(solution)/shard_map/ppermute | solution.py:280
  35.4 44.5 %collective-permute-start.17 = (bf16[24,128,256]{2,1,0:T(8,128)(2,1)S(1)}, bf16[24,128,256]{2,1,0:T(8,128)(2,1)S(1)}, u32[]{:S(2)}, u32[]{:S(2)}) collective-permute-start(bf16[24,128,256]{2,1,0:T(8,128)(2,1)S(1)} %bitcast.15), channel_id=1, source_target_pairs={{0,1},{1,2},{2,3},{3,4},{4,5},{5,6},{6,7},{7,8},{8,9},{9,10},{10,1... | collective-permute-start | bytes 4718600 | tf_op jit(solution)/shard_map/ppermute | solution.py:338
  37.3 11.2 %collective-permute-start.9 = (bf16[4,272,256]{2,1,0:T(8,128)(2,1)S(1)}, bf16[4,272,256]{2,1,0:T(8,128)(2,1)S(1)}, u32[]{:S(2)}, u32[]{:S(2)}) collective-permute-start(bf16[4,272,256]{2,1,0:T(8,128)(2,1)S(1)} %pad_maximum_fusion.refs_0_), channel_id=1, source_target_pairs={{0,1},{1,0},{2,3},{3,2},{4,5},{5,4},{6,7},{7,6},{8,9},{9,8},{10,11... | collective-permute-start | bytes 1671176 | tf_op jit(solution)/shard_map/ppermute | solution.py:245
  37.4 17.8 %collective-permute-start.3 = (bf16[4,272,256]{2,1,0:T(8,128)(2,1)S(1)}, bf16[4,272,256]{2,1,0:T(8,128)(2,1)}, u32[]{:S(2)}, u32[]{:S(2)}) collective-permute-start(bf16[4,272,256]{2,1,0:T(8,128)(2,1)S(1)} %collective-permute-done.2.refs_1_), channel_id=1, source_target_pairs={{0,2},{1,3},{2,4},{3,5},{4,6},{5,7},{6,8},{7,9},{8,10},{9,11},{10,... | collective-permute-start | bytes 1671176 | tf_op jit(solution)/shard_map/ppermute | solution.py:280
  44.7 12.6 %collective-permute-start.7 = (bf16[4,272,256]{2,1,0:T(8,128)(2,1)}, bf16[4,272,256]{2,1,0:T(8,128)(2,1)}, u32[]{:S(2)}, u32[]{:S(2)}) collective-permute-start(bf16[4,272,256]{2,1,0:T(8,128)(2,1)} %collective-permute-done.6.refs_5_), channel_id=1, source_target_pairs={{0,14},{1,15},{2,0},{3,1},{4,2},{5,3},{6,4},{7,5},{8,6},{9,7},{10,... | collective-permute-start | bytes 1671176 | tf_op jit(solution)/shard_map/ppermute | solution.py:280
  48.5 12.5 %collective-permute-start.10 = (bf16[4,272,256]{2,1,0:T(8,128)(2,1)S(1)}, bf16[4,272,256]{2,1,0:T(8,128)(2,1)S(1)}, u32[]{:S(2)}, u32[]{:S(2)}) collective-permute-start(bf16[4,272,256]{2,1,0:T(8,128)(2,1)S(1)} %collective-permute-done.2.refs_1_), channel_id=1, source_target_pairs={{0,1},{1,0},{2,3},{3,2},{4,5},{5,4},{6,7},{7,6},{8,9},{9,8},{10,11... | collective-permute-start | bytes 1671176 | tf_op jit(solution)/shard_map/ppermute | solution.py:245
  48.5 31.3 %collective-permute-start.13 = (bf16[4,272,256]{2,1,0:T(8,128)(2,1)S(1)}, bf16[4,272,256]{2,1,0:T(8,128)(2,1)S(1)}, u32[]{:S(2)}, u32[]{:S(2)}) collective-permute-start(bf16[4,272,256]{2,1,0:T(8,128)(2,1)S(1)} %collective-permute-done.5.refs_4_), channel_id=1, source_target_pairs={{0,1},{1,0},{2,3},{3,2},{4,5},{5,4},{6,7},{7,6},{8,9},{9,8},{10,11... | collective-permute-start | bytes 1671176 | tf_op jit(solution)/shard_map/ppermute | solution.py:245
  55.3 26.2 %collective-permute-start.4 = (bf16[4,272,256]{2,1,0:T(8,128)(2,1)}, bf16[4,272,256]{2,1,0:T(8,128)(2,1)}, u32[]{:S(2)}, u32[]{:S(2)}) collective-permute-start(bf16[4,272,256]{2,1,0:T(8,128)(2,1)} %collective-permute-done.3.refs_2_), channel_id=1, source_target_pairs={{0,2},{1,3},{2,4},{3,5},{4,6},{5,7},{6,8},{7,9},{8,10},{9,11},{10,... | collective-permute-start | bytes 1671176 | tf_op jit(solution)/shard_map/ppermute | solution.py:280
  57.3 29.7 %collective-permute-start.8 = (bf16[4,272,256]{2,1,0:T(8,128)(2,1)}, bf16[4,272,256]{2,1,0:T(8,128)(2,1)}, u32[]{:S(2)}, u32[]{:S(2)}) collective-permute-start(bf16[4,272,256]{2,1,0:T(8,128)(2,1)} %collective-permute-done.7.refs_6_), channel_id=1, source_target_pairs={{0,14},{1,15},{2,0},{3,1},{4,2},{5,3},{6,4},{7,5},{8,6},{9,7},{10,... | collective-permute-start | bytes 1671176 | tf_op jit(solution)/shard_map/ppermute | solution.py:280
  61.0 29.1 %collective-permute-start.11 = (bf16[4,272,256]{2,1,0:T(8,128)(2,1)}, bf16[4,272,256]{2,1,0:T(8,128)(2,1)}, u32[]{:S(2)}, u32[]{:S(2)}) collective-permute-start(bf16[4,272,256]{2,1,0:T(8,128)(2,1)} %collective-permute-done.3.refs_2_), channel_id=1, source_target_pairs={{0,1},{1,0},{2,3},{3,2},{4,5},{5,4},{6,7},{7,6},{8,9},{9,8},{10,11... | collective-permute-start | bytes 1671176 | tf_op jit(solution)/shard_map/ppermute | solution.py:245
  79.8 10.3 %collective-permute-start.14 = (bf16[4,272,256]{2,1,0:T(8,128)(2,1)}, bf16[4,272,256]{2,1,0:T(8,128)(2,1)}, u32[]{:S(2)}, u32[]{:S(2)}) collective-permute-start(bf16[4,272,256]{2,1,0:T(8,128)(2,1)} %collective-permute-done.6.refs_5_), channel_id=1, source_target_pairs={{0,1},{1,0},{2,3},{3,2},{4,5},{5,4},{6,7},{7,6},{8,9},{9,8},{10,11... | collective-permute-start | bytes 1671176 | tf_op jit(solution)/shard_map/ppermute | solution.py:245
  81.1 9.0 %collective-permute-start.15 = (bf16[4,272,256]{2,1,0:T(8,128)(2,1)}, bf16[4,272,256]{2,1,0:T(8,128)(2,1)S(1)}, u32[]{:S(2)}, u32[]{:S(2)}) collective-permute-start(bf16[4,272,256]{2,1,0:T(8,128)(2,1)} %collective-permute-done.7.refs_6_), channel_id=1, source_target_pairs={{0,1},{1,0},{2,3},{3,2},{4,5},{5,4},{6,7},{7,6},{8,9},{9,8},{10,11... | collective-permute-start | bytes 1671176 | tf_op jit(solution)/shard_map/ppermute | solution.py:245
  81.5 8.6 %collective-permute-start.12 = (bf16[4,272,256]{2,1,0:T(8,128)(2,1)}, bf16[4,272,256]{2,1,0:T(8,128)(2,1)S(1)}, u32[]{:S(2)}, u32[]{:S(2)}) collective-permute-start(bf16[4,272,256]{2,1,0:T(8,128)(2,1)} %collective-permute-done.4.refs_3_), channel_id=1, source_target_pairs={{0,1},{1,0},{2,3},{3,2},{4,5},{5,4},{6,7},{7,6},{8,9},{9,8},{10,11... | collective-permute-start | bytes 1671176 | tf_op jit(solution)/shard_map/ppermute | solution.py:245
  153.5 8.4 %collective-permute-start.19 = (f32[256,256]{1,0:T(8,128)S(1)}, f32[256,256]{1,0:T(8,128)S(1)}, u32[]{:S(2)}, u32[]{:S(2)}) collective-permute-start(f32[256,256]{1,0:T(8,128)S(1)} %constant_dynamic-slice_fusion.3), channel_id=1, source_target_pairs={{0,16},{1,17},{2,18},{3,19},{4,20},{5,21},{6,22},{7,23},{8,24},{9,... | collective-permute-start | bytes 786440 | tf_op jit(solution)/shard_map/ppermute | solution.py:245
  162.0 5.2 %collective-permute-start.20 = (f32[128,256]{1,0:T(8,128)S(1)}, f32[128,256]{1,0:T(8,128)S(1)}, u32[]{:S(2)}, u32[]{:S(2)}) collective-permute-start(f32[128,256]{1,0:T(8,128)S(1)} %constant_dynamic-slice_fusion.2), channel_id=1, source_target_pairs={{0,48},{1,49},{2,50},{3,51},{4,52},{5,53},{6,54},{7,55},{8,56},{9,... | collective-permute-start | bytes 393224 | tf_op jit(solution)/shard_map/ppermute | solution.py:245
  171.6 5.4 %collective-permute-start.22 = (f32[32,256]{1,0:T(8,128)S(1)}, f32[32,256]{1,0:T(8,128)S(1)}, u32[]{:S(2)}, u32[]{:S(2)}) collective-permute-start(f32[32,256]{1,0:T(8,128)S(1)} %constant_dynamic-slice_fusion), channel_id=1, source_target_pairs={{0,4},{1,5},{2,6},{3,7},{4,0},{5,1},{6,2},{7,3},{8,12},{9,13},{10,... | collective-permute-start | bytes 98312 | tf_op jit(solution)/shard_map/ppermute | solution.py:245
  176.9 6.0 %collective-permute-start.23 = (f32[32,256]{1,0:T(8,128)S(1)}, f32[32,256]{1,0:T(8,128)S(1)}, u32[]{:S(2)}, u32[]{:S(2)}) collective-permute-start(f32[32,256]{1,0:T(8,128)S(1)} %dynamic-slice_add_fusion.4), channel_id=1, source_target_pairs={{0,12},{1,13},{2,14},{3,15},{4,8},{5,9},{6,10},{7,11},{8,4},{9,5},... | collective-permute-start | bytes 98312 | tf_op jit(solution)/shard_map/ppermute | solution.py:245
  188.0 5.1 %collective-permute-start.25 = (f32[32,256]{1,0:T(8,128)S(1)}, f32[32,256]{1,0:T(8,128)S(1)}, u32[]{:S(2)}, u32[]{:S(2)}) collective-permute-start(f32[32,256]{1,0:T(8,128)S(1)} %add.146), channel_id=1, source_target_pairs={{0,192},{64,128},{128,64},{192,0},{1,193},{65,129},{129,65},{193,1... | collective-permute-start | bytes 98312 | tf_op jit(solution)/shard_map/ppermute | solution.py:245
  202.3 5.1 %collective-permute-start.28 = (f32[128,256]{1,0:T(8,128)S(1)}, f32[128,256]{1,0:T(8,128)S(1)}, u32[]{:S(2)}, u32[]{:S(2)}) collective-permute-start(f32[128,256]{1,0:T(8,128)S(1)} %maximum_select_fusion.3), channel_id=1, source_target_pairs={{0,48},{1,49},{2,50},{3,51},{4,52},{5,53},{6,54},{7,55},{8,56},{9,... | collective-permute-start | bytes 393224 | tf_op jit(solution)/shard_map/ppermute | solution.py:245
  207.4 8.5 %collective-permute-start.29 = (f32[256,256]{1,0:T(8,128)S(1)}, f32[256,256]{1,0:T(8,128)S(1)}, u32[]{:S(2)}, u32[]{:S(2)}) collective-permute-start(f32[256,256]{1,0:T(8,128)S(1)} %maximum_select_fusion.2), channel_id=1, source_target_pairs={{0,16},{1,17},{2,18},{3,19},{4,20},{5,21},{6,22},{7,23},{8,24},{9,... | collective-permute-start | bytes 786440 | tf_op jit(solution)/shard_map/ppermute | solution.py:245
  (19 other events, 484.8 us)
